TPU v7x, 128 devices: a whole 4x4x4 slice. The times are simulated.
128 devices in a mesh: mem: 8 (over z_lo, y), sp: 16 (over z_hi, x, core).
Axes of the slice: x: 4, y: 4, z: 4 (z_hi: 2, z_lo: 2; z = z_hi * 2 + z_lo), core: 2. Of those that a mesh axis runs over, the one named last changes fastest.
Arguments:
- anomalies: float32 [64, 3, 256, 4096], P('mem', None, 'sp'), may hold values from -6 to 6
- mean_state: float32 [3, 256, 4096], P(None, 'sp'), may hold values from -3 to 3
- weights: float32 [64], replicated, may hold values from -0.4375 to 0.4375
- station_row: int32 [4096], P('sp'), may hold values from 0 to 14
- station_col: int32 [4096], P('sp'), may hold values from 0 to 4095
- stencil_row: int32 [4, 4096], P(None, 'sp'), may hold values from 0 to 1
- stencil_col: int32 [4, 4096], P(None, 'sp'), may hold values from -1 to 1
- obs_weight: float32 [4, 4096], P(None, 'sp'), may hold values from 0.05 to 0.25
- obs_value: float32 [4, 4096], P(None, 'sp'), may hold values from -6 to 6
- obs_var: float32 [4, 4096], P(None, 'sp'), may hold values from 1 to 10
Outputs:
- obs_anom: float32 [64, 4, 4096], P('mem', None, 'sp')
- gradient: float32 [64], replicated
- hessian: float32 [64, 64], replicated
All inputs are finite; a program needn't handle non-finite values.
Results may differ from a plain program's by a relative error of at most 0.0003.
Values sent between devices are 32-bit elements; how exact they have to be, the bound alone decides.
No kernel may reach another device: no remote copies, remote signals or barrier semaphores. Data moves between devices by JAX's collectives and lax.ppermute only.
A program may use at most 192 MiB of HBM per device.

v0:
```python
import jax
import jax.numpy as jnp
from jax import lax
from jax.sharding import PartitionSpec as P

STEPS = 4


time_step = 1.0
coriolis = 0.1
perturb = 0.1


def padded_2(block, sides, width):
    for axis, dim in sides:
        count = lax.axis_size(axis)
        forward = [(i, i + 1) for i in range(count - 1)]
        forward.append((count - 1, 0))
        backward = [(target, source) for source, target in forward]
        low = lax.ppermute(
            lax.slice_in_dim(block, block.shape[dim] - width, None, axis=dim), axis, forward
        )
        high = lax.ppermute(lax.slice_in_dim(block, 0, width, axis=dim), axis, backward)
        block = jnp.concatenate([low, block, high], axis=dim)
    return block


def row_diff(a):
    return (a[:, 2:] - a[:, :-2]) * 0.5


def col_diff(a):
    return (jnp.roll(a, -1, axis=-1) - jnp.roll(a, 1, axis=-1)) * 0.5


def height_update(height, along, across):
    depth = 1.0 + height
    return height[:, 1:-1] - time_step * (
        row_diff(depth * along) + col_diff(depth * across)[:, 1:-1]
    )


def momentum_update(fresh, along, across):
    inner_u = along[:, 1:-1]
    inner_v = across[:, 1:-1]
    new_u = inner_u + time_step * (
        coriolis * inner_v
        - row_diff(fresh)
        - inner_u * row_diff(along)
        - inner_v * col_diff(along)[:, 1:-1]
    )
    new_v = inner_v + time_step * (
        -coriolis * inner_u
        - col_diff(fresh)[:, 1:-1]
        - inner_u * row_diff(across)
        - inner_v * col_diff(across)[:, 1:-1]
    )
    return jnp.stack([fresh[:, 1:-1], new_u, new_v], axis=1)


def observe(height, flat_index, obs_weight):
    flat = height.reshape(height.shape[0], -1)
    picked = jnp.take(flat, flat_index, axis=1)
    return jnp.sum(obs_weight[None] * picked, axis=1)


def body(
    anomalies,
    mean_state,
    weights,
    station_row,
    station_col,
    stencil_row,
    stencil_col,
    obs_weight,
    obs_value,
    obs_var,
):
    members = anomalies.shape[0]
    columns = anomalies.shape[3]
    total = weights.shape[0]
    first = lax.axis_index("mem") * members
    own_weights = lax.dynamic_slice_in_dim(weights, first, members, 0)
    partial_value = jnp.tensordot(own_weights, anomalies, axes=1, precision=lax.Precision.HIGHEST)
    increment = lax.psum(partial_value, "mem")
    centre = mean_state + increment
    state = centre[None] + perturb * anomalies
    flat_index = (station_row[None, :] + stencil_row) * columns + (
        station_col[None, :] + stencil_col
    ) % columns
    seen = []
    for step in range(STEPS):
        padded = padded_2(state, (("sp", 2),), 1)
        fresh = height_update(padded[:, 0], padded[:, 1], padded[:, 2])
        fresh_pad = padded_2(fresh, (("sp", 1),), 1)
        state = momentum_update(fresh_pad, padded[:, 1], padded[:, 2])
        seen.append(observe(state[:, 0], flat_index, obs_weight))
    own_obs = jnp.stack(seen, axis=1)
    gathered = lax.all_gather(own_obs, "mem", axis=0, tiled=True)
    mean_obs = jnp.mean(gathered, axis=0)
    obs_anom = (own_obs - mean_obs) / perturb
    flat_anom = ((gathered - mean_obs) / perturb).reshape(total, -1)
    weighted = flat_anom * (1.0 / obs_var).reshape(-1)
    innov = (obs_value - mean_obs).reshape(-1)
    gram = jnp.dot(weighted, flat_anom.T, precision=lax.Precision.HIGHEST)
    pull = jnp.dot(weighted, innov, precision=lax.Precision.HIGHEST)
    gram, pull = lax.psum((gram, pull), "sp")
    hessian = gram + (total - 1) * jnp.eye(total, dtype=jnp.float32)
    gradient = (total - 1) * weights - pull
    return (obs_anom, gradient, hessian)


def solution(mesh):
    return jax.shard_map(
        body,
        mesh=mesh,
        in_specs=(
            P("mem", None, "sp", None),
            P(None, "sp", None),
            P(),
            P("sp"),
            P("sp"),
            P(None, "sp"),
            P(None, "sp"),
            P(None, "sp"),
            P(None, "sp"),
            P(None, "sp"),
        ),
        out_specs=(P("mem", None, "sp"), P(), P()),
        check_vma=False,
    )
```

profile of v0, /device:TPU:0, one launch (start us, length us, event | category | flops | bytes accessed | tf_op | source)
XLA Modules:
  0.0 450.2 jit_solution(12270124455747146730)
XLA Ops:
  7.2 11.4 %fusion = f32[1,3,16,4096]{3,0,2,1:T(1,128)S(1)} fusion(f32[8,3,16,4096]{3,2,1,0:T(8,128)} %param.12, f32[64]{0:T(128)} %param.14, s32[]{:T(128)S(6)} %select_n.17), kind=kOutput, calls=%fused_computation.9 | convolution fusion | flops 18874368 | bytes 7078148 | tf_op jit(solution)/shard_map/dot_general | solution.py:84
  20.0 78.6 %all-reduce.3.cloned.1.call-done = f32[3,16,4096]{2,1,0:T(8,128)} async-done(((f32[3,16,4096]{2,1,0:T(8,128)}), f32[3,16,4096]{2,1,0:T(8,128)}) %all-reduce.3.cloned.1.call-update) | async-done | bytes 786448 | tf_op jit(solution)/shard_map/psum | solution.py:85
  99.8 7.0 %multiply_add_fusion = f32[8,3,16,4096]{3,0,2,1:T(8,128)S(1)} fusion(f32[8,3,16,4096]{3,2,1,0:T(8,128)} %param.12, f32[3,16,4096]{2,1,0:T(8,128)S(1)} %add.97), kind=kLoop, calls=%fused_computation.8 | loop fusion | flops 3145728 | bytes 13369344 | tf_op jit(solution)/shard_map/add | solution.py:87
  106.9 5.5 %collective-permute-start.1 = (f32[8,3,1,4096]{3,0,2,1:T(8,128)S(1)}, f32[8,3,1,4096]{3,0,2,1:T(8,128)S(1)}, u32[]{:S(2)}, u32[]{:S(2)}) collective-permute-start(f32[8,3,1,4096]{3,0,2,1:T(8,128)S(1)} %get-tuple-element.42), channel_id=1, source_target_pairs={{1,0},{2,1},{3,2},{4,3},{5,4},{6,5},{7,6},{8,7},{9,8},{10,9},{11,1... | collective-permute-start | bytes 1179656 | tf_op jit(solution)/shard_map/ppermute | solution.py:23
  112.4 5.3 %collective-permute-done = f32[8,3,1,4096]{3,0,2,1:T(8,128)S(1)} collective-permute-done((f32[8,3,1,4096]{3,0,2,1:T(8,128)S(1)}, f32[8,3,1,4096]{3,0,2,1:T(8,128)S(1)}, u32[]{:S(2)}, u32[]{:S(2)}) %collective-permute-start) | collective-permute-done | bytes 393248 | tf_op jit(solution)/shard_map/ppermute | solution.py:20
  121.3 5.6 %collective-permute-start.2 = (f32[8,1,4096]{2,0,1:T(8,128)S(1)}, f32[8,1,4096]{2,0,1:T(8,128)S(1)}, u32[]{:S(2)}, u32[]{:S(2)}) collective-permute-start(f32[8,1,4096]{2,0,1:T(8,128)S(1)} %get-tuple-element.94), channel_id=1, source_target_pairs={{1,0},{2,1},{3,2},{4,3},{5,4},{6,5},{7,6},{8,7},{9,8},{10,9},{11,1... | collective-permute-start | bytes 393224 | tf_op jit(solution)/shard_map/ppermute | solution.py:23
  126.8 3.2 fusion.134
  130.1 4.7 %collective-permute-done.3 = f32[8,1,4096]{2,0,1:T(8,128)S(1)} collective-permute-done((f32[8,1,4096]{2,0,1:T(8,128)S(1)}, f32[8,1,4096]{2,0,1:T(8,128)S(1)}, u32[]{:S(2)}, u32[]{:S(2)}) %collective-permute-start.3) | collective-permute-done | bytes 131104 | tf_op jit(solution)/shard_map/ppermute | solution.py:20
  136.7 2.2 fusion.84
  138.9 2.8 fusion.72
  141.9 5.5 %collective-permute-start.5 = (f32[8,3,1,4096]{3,0,2,1:T(8,128)S(1)}, f32[8,3,1,4096]{3,0,2,1:T(8,128)S(1)}, u32[]{:S(2)}, u32[]{:S(2)}) collective-permute-start(f32[8,3,1,4096]{3,0,2,1:T(8,128)S(1)} %get-tuple-element.40), channel_id=1, source_target_pairs={{1,0},{2,1},{3,2},{4,3},{5,4},{6,5},{7,6},{8,7},{9,8},{10,9},{11,1... | collective-permute-start | bytes 1179656 | tf_op jit(solution)/shard_map/ppermute | solution.py:23
  147.4 5.3 %collective-permute-done.4 = f32[8,3,1,4096]{3,0,2,1:T(8,128)S(1)} collective-permute-done((f32[8,3,1,4096]{3,0,2,1:T(8,128)S(1)}, f32[8,3,1,4096]{3,0,2,1:T(8,128)S(1)}, u32[]{:S(2)}, u32[]{:S(2)}) %collective-permute-start.4) | collective-permute-done | bytes 393248 | tf_op jit(solution)/shard_map/ppermute | solution.py:20
  157.6 5.6 %collective-permute-start.6 = (f32[8,1,4096]{2,0,1:T(8,128)S(1)}, f32[8,1,4096]{2,0,1:T(8,128)S(1)}, u32[]{:S(2)}, u32[]{:S(2)}) collective-permute-start(f32[8,1,4096]{2,0,1:T(8,128)S(1)} %get-tuple-element.92), channel_id=1, source_target_pairs={{1,0},{2,1},{3,2},{4,3},{5,4},{6,5},{7,6},{8,7},{9,8},{10,9},{11,1... | collective-permute-start | bytes 393224 | tf_op jit(solution)/shard_map/ppermute | solution.py:23
  165.7 5.5 %collective-permute-done.7 = f32[8,1,4096]{2,0,1:T(8,128)S(1)} collective-permute-done((f32[8,1,4096]{2,0,1:T(8,128)S(1)}, f32[8,1,4096]{2,0,1:T(8,128)S(1)}, u32[]{:S(2)}, u32[]{:S(2)}) %collective-permute-start.7) | collective-permute-done | bytes 131104 | tf_op jit(solution)/shard_map/ppermute | solution.py:20
  174.4 2.8 fusion.43
  177.4 5.6 %collective-permute-start.9 = (f32[8,3,1,4096]{3,0,2,1:T(8,128)S(1)}, f32[8,3,1,4096]{3,0,2,1:T(8,128)S(1)}, u32[]{:S(2)}, u32[]{:S(2)}) collective-permute-start(f32[8,3,1,4096]{3,0,2,1:T(8,128)S(1)} %get-tuple-element.38), channel_id=1, source_target_pairs={{1,0},{2,1},{3,2},{4,3},{5,4},{6,5},{7,6},{8,7},{9,8},{10,9},{11,1... | collective-permute-start | bytes 1179656 | tf_op jit(solution)/shard_map/ppermute | solution.py:23
  183.0 5.2 %collective-permute-done.8 = f32[8,3,1,4096]{3,0,2,1:T(8,128)S(1)} collective-permute-done((f32[8,3,1,4096]{3,0,2,1:T(8,128)S(1)}, f32[8,3,1,4096]{3,0,2,1:T(8,128)S(1)}, u32[]{:S(2)}, u32[]{:S(2)}) %collective-permute-start.8) | collective-permute-done | bytes 393248 | tf_op jit(solution)/shard_map/ppermute | solution.py:20
  195.2 5.6 %collective-permute-start.10 = (f32[8,1,4096]{2,0,1:T(8,128)S(1)}, f32[8,1,4096]{2,0,1:T(8,128)S(1)}, u32[]{:S(2)}, u32[]{:S(2)}) collective-permute-start(f32[8,1,4096]{2,0,1:T(8,128)S(1)} %get-tuple-element.90), channel_id=1, source_target_pairs={{1,0},{2,1},{3,2},{4,3},{5,4},{6,5},{7,6},{8,7},{9,8},{10,9},{11,1... | collective-permute-start | bytes 393224 | tf_op jit(solution)/shard_map/ppermute | solution.py:23
  203.3 5.5 %collective-permute-done.11 = f32[8,1,4096]{2,0,1:T(8,128)S(1)} collective-permute-done((f32[8,1,4096]{2,0,1:T(8,128)S(1)}, f32[8,1,4096]{2,0,1:T(8,128)S(1)}, u32[]{:S(2)}, u32[]{:S(2)}) %collective-permute-start.11) | collective-permute-done | bytes 131104 | tf_op jit(solution)/shard_map/ppermute | solution.py:20
  212.0 2.8 fusion.14
  216.4 5.6 %collective-permute-start.13 = (f32[8,3,1,4096]{3,0,2,1:T(8,128)}, f32[8,3,1,4096]{3,0,2,1:T(8,128)}, u32[]{:S(2)}, u32[]{:S(2)}) collective-permute-start(f32[8,3,1,4096]{3,0,2,1:T(8,128)} %get-tuple-element.36), channel_id=1, source_target_pairs={{1,0},{2,1},{3,2},{4,3},{5,4},{6,5},{7,6},{8,7},{9,8},{10,9},{11,1... | collective-permute-start | bytes 1179656 | tf_op jit(solution)/shard_map/ppermute | solution.py:23
  222.1 15.6 %copy.29 = f32[8,16,4096]{0,2,1:T(8,128)} copy(f32[8,16,4096]{2,0,1:T(8,128)S(1)} %fusion.94) | data formatting | bytes 4194304 | tf_op jit(solution)/shard_map/sub | solution.py:38
  237.6 13.3 %gather_fusion = f32[1024,8]{1,0:T(8,128)S(1)} fusion(f32[8,65536]{0,1:T(8,128)} %bitcast.122, s32[1024]{0:T(1024)S(1)} %broadcast_clamp_fusion), kind=kCustom, calls=%fused_computation.clone | custom fusion | bytes 69632 | tf_op jit(solution)/shard_map/jit(_take)/gather | solution.py:63
  251.0 16.4 %copy.31 = f32[8,16,4096]{0,2,1:T(8,128)} copy(f32[8,16,4096]{2,0,1:T(8,128)} %copy-done) | data formatting | bytes 4194304 | tf_op jit(solution)/shard_map/sub | solution.py:38
  267.4 13.3 %gather_fusion.1 = f32[1024,8]{1,0:T(8,128)S(1)} fusion(f32[8,65536]{0,1:T(8,128)} %bitcast.123, s32[1024]{0:T(1024)S(1)} %broadcast_clamp_fusion), kind=kCustom, calls=%fused_computation.1.clone | custom fusion | bytes 69632 | tf_op jit(solution)/shard_map/jit(_take)/gather | solution.py:63
  280.8 15.6 %copy.33 = f32[8,16,4096]{0,2,1:T(8,128)} copy(f32[8,16,4096]{2,0,1:T(8,128)S(1)} %copy-done.2) | data formatting | bytes 4194304 | tf_op jit(solution)/shard_map/sub | solution.py:38
  296.3 14.5 %gather_fusion.2 = f32[1024,8]{1,0:T(8,128)} fusion(f32[8,65536]{0,1:T(8,128)} %bitcast.124, s32[1024]{0:T(1024)S(1)} %broadcast_clamp_fusion), kind=kCustom, calls=%fused_computation.2.clone | custom fusion | bytes 69632 | tf_op jit(solution)/shard_map/jit(_take)/gather | solution.py:63
  310.9 2.6 pad_maximum_fusion.3
  316.2 15.6 %copy.35 = f32[8,16,4096]{0,2,1:T(8,128)} copy(f32[8,16,4096]{2,0,1:T(8,128)S(1)} %fusion.7) | data formatting | bytes 4194304 | tf_op jit(solution)/shard_map/sub | solution.py:38
  331.8 13.4 %gather_fusion.3 = f32[1024,8]{1,0:T(8,128)S(1)} fusion(f32[8,65536]{0,1:T(8,128)} %bitcast.121, s32[1024]{0:T(1024)S(1)} %broadcast_clamp_fusion), kind=kCustom, calls=%fused_computation.3.clone | custom fusion | bytes 69632 | tf_op jit(solution)/shard_map/jit(_take)/gather | solution.py:63
  346.9 28.4 %all_gather.3 = f32[64,4,256]{2,0,1:T(8,128)S(1)} all-gather(f32[8,4,256]{2,0,1:T(8,128)S(1)} %pad_maximum_fusion.60), channel_id=1, replica_groups=mesh['mem'=8,'sp'=16] {'mem'}, dimensions={0}, use_global_device_ids=true | all-gather | bytes 294912 | tf_op jit(solution)/shard_map/all_gather | solution.py:99
  376.0 65.0 %all-reduce = (f32[64]{0:T(128)S(1)}, f32[64,64]{1,0:T(8,128)S(1)}) all-reduce(f32[64]{0:T(128)S(1)} %convolution_bitcast_fusion.1, f32[64,64]{1,0:T(8,128)S(1)} %convolution_bitcast_fusion), channel_id=1, replica_groups=mesh['mem'=8,'sp'=16] {'sp'}, use_global_device_ids=true, to_apply=%region_6.8 | all-reduce | flops 4160 | bytes 33280 | tf_op jit(solution)/shard_map/psum | solution.py:107
  (116 shorter events, 40.1 us)
Async XLA Ops:
  7.2 91.4 %all-reduce.3.cloned.1.call-start = ((), (), s32[]{:S(2)}) async-start(), calls=%async_computation | async-start | bytes 1572864 | tf_op jit(solution)/shard_map/psum | solution.py:85
  18.6 80.0 %copy-start.7 = (f32[3,16,4096]{2,1,0:T(8,128)S(1)}, f32[3,16,4096]{2,1,0:T(8,128)}, u32[]{:S(2)}) copy-start(f32[3,16,4096]{2,1,0:T(8,128)} %param.13) | copy-start | bytes 2359300
  106.8 10.9 %collective-permute-start = (f32[8,3,1,4096]{3,0,2,1:T(8,128)S(1)}, f32[8,3,1,4096]{3,0,2,1:T(8,128)S(1)}, u32[]{:S(2)}, u32[]{:S(2)}) collective-permute-start(f32[8,3,1,4096]{3,0,2,1:T(8,128)S(1)} %get-tuple-element.41), channel_id=1, source_target_pairs={{0,1},{1,2},{2,3},{3,4},{4,5},{5,6},{6,7},{7,8},{8,9},{9,10},{10,1... | collective-permute-start | bytes 1179656 | tf_op jit(solution)/shard_map/ppermute | solution.py:20
  106.9 10.8 %collective-permute-start.1 = (f32[8,3,1,4096]{3,0,2,1:T(8,128)S(1)}, f32[8,3,1,4096]{3,0,2,1:T(8,128)S(1)}, u32[]{:S(2)}, u32[]{:S(2)}) collective-permute-start(f32[8,3,1,4096]{3,0,2,1:T(8,128)S(1)} %get-tuple-element.42), channel_id=1, source_target_pairs={{1,0},{2,1},{3,2},{4,3},{5,4},{6,5},{7,6},{8,7},{9,8},{10,9},{11,1... | collective-permute-start | bytes 1179656 | tf_op jit(solution)/shard_map/ppermute | solution.py:23
  121.3 8.9 %collective-permute-start.2 = (f32[8,1,4096]{2,0,1:T(8,128)S(1)}, f32[8,1,4096]{2,0,1:T(8,128)S(1)}, u32[]{:S(2)}, u32[]{:S(2)}) collective-permute-start(f32[8,1,4096]{2,0,1:T(8,128)S(1)} %get-tuple-element.94), channel_id=1, source_target_pairs={{1,0},{2,1},{3,2},{4,3},{5,4},{6,5},{7,6},{8,7},{9,8},{10,9},{11,1... | collective-permute-start | bytes 393224 | tf_op jit(solution)/shard_map/ppermute | solution.py:23
  126.8 8.0 %collective-permute-start.3 = (f32[8,1,4096]{2,0,1:T(8,128)S(1)}, f32[8,1,4096]{2,0,1:T(8,128)S(1)}, u32[]{:S(2)}, u32[]{:S(2)}) collective-permute-start(f32[8,1,4096]{2,0,1:T(8,128)S(1)} %get-tuple-element.93), channel_id=1, source_target_pairs={{0,1},{1,2},{2,3},{3,4},{4,5},{5,6},{6,7},{7,8},{8,9},{9,10},{10,1... | collective-permute-start | bytes 393224 | tf_op jit(solution)/shard_map/ppermute | solution.py:20
  135.0 1.7 copy-start.5
  141.8 10.9 %collective-permute-start.4 = (f32[8,3,1,4096]{3,0,2,1:T(8,128)S(1)}, f32[8,3,1,4096]{3,0,2,1:T(8,128)S(1)}, u32[]{:S(2)}, u32[]{:S(2)}) collective-permute-start(f32[8,3,1,4096]{3,0,2,1:T(8,128)S(1)} %get-tuple-element.39), channel_id=1, source_target_pairs={{0,1},{1,2},{2,3},{3,4},{4,5},{5,6},{6,7},{7,8},{8,9},{9,10},{10,1... | collective-permute-start | bytes 1179656 | tf_op jit(solution)/shard_map/ppermute | solution.py:20
  141.9 10.8 %collective-permute-start.5 = (f32[8,3,1,4096]{3,0,2,1:T(8,128)S(1)}, f32[8,3,1,4096]{3,0,2,1:T(8,128)S(1)}, u32[]{:S(2)}, u32[]{:S(2)}) collective-permute-start(f32[8,3,1,4096]{3,0,2,1:T(8,128)S(1)} %get-tuple-element.40), channel_id=1, source_target_pairs={{1,0},{2,1},{3,2},{4,3},{5,4},{6,5},{7,6},{8,7},{9,8},{10,9},{11,1... | collective-permute-start | bytes 1179656 | tf_op jit(solution)/shard_map/ppermute | solution.py:23
  157.5 30.8 %copy-start = (f32[8,16,4096]{2,0,1:T(8,128)}, f32[8,16,4096]{2,0,1:T(8,128)S(1)}, u32[]{:S(2)}) copy-start(f32[8,16,4096]{2,0,1:T(8,128)S(1)} %fusion.65) | copy-start | bytes 6291460
  157.6 8.1 %collective-permute-start.6 = (f32[8,1,4096]{2,0,1:T(8,128)S(1)}, f32[8,1,4096]{2,0,1:T(8,128)S(1)}, u32[]{:S(2)}, u32[]{:S(2)}) collective-permute-start(f32[8,1,4096]{2,0,1:T(8,128)S(1)} %get-tuple-element.92), channel_id=1, source_target_pairs={{1,0},{2,1},{3,2},{4,3},{5,4},{6,5},{7,6},{8,7},{9,8},{10,9},{11,1... | collective-permute-start | bytes 393224 | tf_op jit(solution)/shard_map/ppermute | solution.py:23
  163.2 8.0 %collective-permute-start.7 = (f32[8,1,4096]{2,0,1:T(8,128)S(1)}, f32[8,1,4096]{2,0,1:T(8,128)S(1)}, u32[]{:S(2)}, u32[]{:S(2)}) collective-permute-start(f32[8,1,4096]{2,0,1:T(8,128)S(1)} %get-tuple-element.91), channel_id=1, source_target_pairs={{0,1},{1,2},{2,3},{3,4},{4,5},{5,6},{6,7},{7,8},{8,9},{9,10},{10,1... | collective-permute-start | bytes 393224 | tf_op jit(solution)/shard_map/ppermute | solution.py:20
  177.2 5.8 %copy-start.10 = (s32[4,256]{1,0:T(4,128)S(1)}, s32[4,256]{1,0:T(4,128)}, u32[]{:S(2)}) copy-start(s32[4,256]{1,0:T(4,128)} %param.18) | copy-start | bytes 12292
  177.2 5.8 %copy-start.11 = (s32[4,256]{1,0:T(4,128)S(1)}, s32[4,256]{1,0:T(4,128)}, u32[]{:S(2)}) copy-start(s32[4,256]{1,0:T(4,128)} %param.17) | copy-start | bytes 12292
  177.2 5.8 %copy-start.13 = (s32[256]{0:T(256)S(1)}, s32[256]{0:T(256)}, u32[]{:S(2)}) copy-start(s32[256]{0:T(256)} %param.16) | copy-start | bytes 3076
  177.2 5.7 %copy-start.14 = (s32[256]{0:T(256)S(1)}, s32[256]{0:T(256)}, u32[]{:S(2)}) copy-start(s32[256]{0:T(256)} %param.15) | copy-start | bytes 3076
  177.3 10.9 %collective-permute-start.8 = (f32[8,3,1,4096]{3,0,2,1:T(8,128)S(1)}, f32[8,3,1,4096]{3,0,2,1:T(8,128)S(1)}, u32[]{:S(2)}, u32[]{:S(2)}) collective-permute-start(f32[8,3,1,4096]{3,0,2,1:T(8,128)S(1)} %get-tuple-element.37), channel_id=1, source_target_pairs={{0,1},{1,2},{2,3},{3,4},{4,5},{5,6},{6,7},{7,8},{8,9},{9,10},{10,1... | collective-permute-start | bytes 1179656 | tf_op jit(solution)/shard_map/ppermute | solution.py:20
  177.4 10.9 %collective-permute-start.9 = (f32[8,3,1,4096]{3,0,2,1:T(8,128)S(1)}, f32[8,3,1,4096]{3,0,2,1:T(8,128)S(1)}, u32[]{:S(2)}, u32[]{:S(2)}) collective-permute-start(f32[8,3,1,4096]{3,0,2,1:T(8,128)S(1)} %get-tuple-element.38), channel_id=1, source_target_pairs={{1,0},{2,1},{3,2},{4,3},{5,4},{6,5},{7,6},{8,7},{9,8},{10,9},{11,1... | collective-permute-start | bytes 1179656 | tf_op jit(solution)/shard_map/ppermute | solution.py:23
  192.6 1.7 copy-start.6
  195.1 19.7 %copy-start.1 = (f32[8,16,4096]{2,0,1:T(8,128)}, f32[8,16,4096]{2,0,1:T(8,128)S(1)}, u32[]{:S(2)}) copy-start(f32[8,16,4096]{2,0,1:T(8,128)S(1)} %fusion.36) | copy-start | bytes 6291460
  195.2 8.1 %collective-permute-start.10 = (f32[8,1,4096]{2,0,1:T(8,128)S(1)}, f32[8,1,4096]{2,0,1:T(8,128)S(1)}, u32[]{:S(2)}, u32[]{:S(2)}) collective-permute-start(f32[8,1,4096]{2,0,1:T(8,128)S(1)} %get-tuple-element.90), channel_id=1, source_target_pairs={{1,0},{2,1},{3,2},{4,3},{5,4},{6,5},{7,6},{8,7},{9,8},{10,9},{11,1... | collective-permute-start | bytes 393224 | tf_op jit(solution)/shard_map/ppermute | solution.py:23
  200.8 8.0 %collective-permute-start.11 = (f32[8,1,4096]{2,0,1:T(8,128)S(1)}, f32[8,1,4096]{2,0,1:T(8,128)S(1)}, u32[]{:S(2)}, u32[]{:S(2)}) collective-permute-start(f32[8,1,4096]{2,0,1:T(8,128)S(1)} %get-tuple-element.89), channel_id=1, source_target_pairs={{0,1},{1,2},{2,3},{3,4},{4,5},{5,6},{6,7},{7,8},{8,9},{9,10},{10,1... | collective-permute-start | bytes 393224 | tf_op jit(solution)/shard_map/ppermute | solution.py:20
  212.0 2.9 copy-start.3
  214.8 1.6 copy-start.4
  214.9 7.2 %copy-start.9 = (f32[4,256]{1,0:T(4,128)S(1)}, f32[4,256]{1,0:T(4,128)}, u32[]{:S(2)}) copy-start(f32[4,256]{1,0:T(4,128)} %param.21) | copy-start | bytes 12292
  216.4 94.4 %collective-permute-start.12 = (f32[8,3,1,4096]{3,0,2,1:T(8,128)}, f32[8,3,1,4096]{3,0,2,1:T(8,128)S(1)}, u32[]{:S(2)}, u32[]{:S(2)}) collective-permute-start(f32[8,3,1,4096]{3,0,2,1:T(8,128)} %get-tuple-element.35), channel_id=1, source_target_pairs={{0,1},{1,2},{2,3},{3,4},{4,5},{5,6},{6,7},{7,8},{8,9},{9,10},{10,1... | collective-permute-start | bytes 1179656 | tf_op jit(solution)/shard_map/ppermute | solution.py:20
  216.4 94.4 %collective-permute-start.13 = (f32[8,3,1,4096]{3,0,2,1:T(8,128)}, f32[8,3,1,4096]{3,0,2,1:T(8,128)}, u32[]{:S(2)}, u32[]{:S(2)}) collective-permute-start(f32[8,3,1,4096]{3,0,2,1:T(8,128)} %get-tuple-element.36), channel_id=1, source_target_pairs={{1,0},{2,1},{3,2},{4,3},{5,4},{6,5},{7,6},{8,7},{9,8},{10,9},{11,1... | collective-permute-start | bytes 1179656 | tf_op jit(solution)/shard_map/ppermute | solution.py:23
  251.0 29.8 %copy-start.2 = (f32[8,16,4096]{2,0,1:T(8,128)S(1)}, f32[8,16,4096]{2,0,1:T(8,128)}, u32[]{:S(2)}) copy-start(f32[8,16,4096]{2,0,1:T(8,128)} %copy-done.1) | copy-start | bytes 6291460
  316.2 29.0 %copy-start.8 = (f32[4,256]{1,0:T(4,128)S(1)}, f32[4,256]{1,0:T(4,128)}, u32[]{:S(2)}) copy-start(f32[4,256]{1,0:T(4,128)} %param.19) | copy-start | bytes 12292
  331.8 43.5 %copy-start.12 = (f32[4,256]{1,0:T(4,128)S(1)}, f32[4,256]{1,0:T(4,128)}, u32[]{:S(2)}) copy-start(f32[4,256]{1,0:T(4,128)} %param.20) | copy-start | bytes 12292
  345.2 96.5 %copy-start.15 = (f32[64]{0:T(128)S(1)}, f32[64]{0:T(128)}, u32[]{:S(2)}) copy-start(f32[64]{0:T(128)} %param.14) | copy-start | bytes 772
Sparse Core Ops, SparseCore 0:
  20.1 78.3 all-reduce.2
where the time goes:
time: 459 us; the launch traced here: 450 us
  local copies, waits for them, and re-layouts  139 us (30%)
  waiting for transfers between devices  113 us (25%)
  blocking collectives  93.4 us (20%)
  starting transfers between devices  39.3 us (9%)
  other arithmetic  38.2 us (8%)
  between operations  15.1 us (3%)
  matrix products  12 us (3%)
    psum x1, waiting for transfers between devices, body(): increment = lax.psum(partial_value, 'mem')  78.6 us
    psum x1, blocking collectives, body(): gram, pull = lax.psum((gram, pull), 'sp')  65 us
    sub x4, local copies, waits for them, and re-layouts, height_update(): height[:, 1:-1]  63.1 us
    gather x4, local copies, waits for them, and re-layouts, observe(): picked = jnp.take(flat, flat_index, axis=1)  54.6 us
    ppermute x7, starting transfers between devices, padded_2(): lax.ppermute(lax.slice_in_dim(block, 0, width, axis=dim), axis, backward)  39 us
    ppermute x7, waiting for transfers between devices, padded_2(): lax.ppermute(lax.slice_in_dim(block, block.shape[dim] - width, None, axis...  31.4 us
    all_gather x1, blocking collectives, body(): gathered = lax.all_gather(own_obs, 'mem', axis=0, tiled=True)  28.4 us
    another operation x6, other arithmetic, momentum_update(): return jnp.stack([fresh[:, 1:-1], new_u, new_v], axis=1)  15.1 us
  transfers between devices with their start and end apart: 15, of which 10 were waited for; matrix products, arithmetic and copies ran while one was open for 21% of the time, Pallas kernels for 0%

commit v1 on v0

v1 whole, which is shorter than its diff:
```python
import jax
import jax.numpy as jnp
from jax import lax
from jax.experimental import pallas as pl
from jax.experimental.pallas import tpu as pltpu
from jax.sharding import PartitionSpec as P

STEPS = 4
HALO = 2 * STEPS - 1
LANES = 128

time_step = 1.0
coriolis = 0.1
perturb = 0.1


def ring(axis, step):
    count = lax.axis_size(axis)
    return [(i, (i + step) % count) for i in range(count)]


def prepare_kernel(place, weights, anom, turned, top, bottom, partial):
    members, rows = anom.shape[0], anom.shape[2]
    chunks, width = partial.shape[0], partial.shape[3]
    first = place[0] * members
    scales = [weights[first + m] for m in range(members)]

    def column(t, carry):
        at = pl.ds(pl.multiple_of(t * LANES, LANES), LANES)
        block = anom[:, 0, :, at]
        turned[0, :, :, at] = jnp.swapaxes(block, 0, 1)
        total = scales[0] * block[0]
        for m in range(1, members):
            total = total + scales[m] * block[m]
        per = width // LANES
        inner = pl.ds(pl.multiple_of((t % per) * LANES, LANES), LANES)
        partial[t // per, 0, :, inner] = total
        return carry

    lax.fori_loop(0, anom.shape[3] // LANES, column, 0)

    @pl.when(pl.program_id(1) == 0)
    def _():
        top[0] = turned[0, :HALO]

    @pl.when(pl.program_id(1) == 1)
    def _():
        bottom[0] = turned[0, rows - HALO :]


def prepare(place, weights, anomalies):
    members, fields, rows, columns = anomalies.shape
    half = rows // 2
    chunks = lax.axis_size("mem")
    width = columns // chunks
    smem = pl.BlockSpec(memory_space=pltpu.SMEM)
    edge = pl.BlockSpec((1, HALO, members, columns), lambda f, r: (f, 0, 0, 0))
    return pl.pallas_call(
        prepare_kernel,
        grid=(fields, 2),
        in_specs=[smem, smem, pl.BlockSpec((members, 1, half, columns), lambda f, r: (0, f, r, 0))],
        out_specs=[
            pl.BlockSpec((1, half, members, columns), lambda f, r: (f, r, 0, 0)),
            edge,
            edge,
            pl.BlockSpec((chunks, 1, half, width), lambda f, r: (0, f, r, 0)),
        ],
        out_shape=[
            jax.ShapeDtypeStruct((fields, rows, members, columns), jnp.float32),
            jax.ShapeDtypeStruct((fields, HALO, members, columns), jnp.float32),
            jax.ShapeDtypeStruct((fields, HALO, members, columns), jnp.float32),
            jax.ShapeDtypeStruct((chunks, fields, rows, width), jnp.float32),
        ],
        compiler_params=pltpu.CompilerParams(vmem_limit_bytes=40 << 20),
        name="prepare",
    )(place, weights, anomalies)


def model_kernel(
    spots, turns, low_c, centre, high_c, obs_weight, own, low, high, out, state, heights, spare, sems
):
    rows, columns = own.shape[1], own.shape[3]
    tiles = columns // LANES
    tall = rows + 2 * HALO
    copies = [
        pltpu.make_async_copy(low, state.at[:, pl.ds(0, HALO)], sems.at[0]),
        pltpu.make_async_copy(own, state.at[:, pl.ds(HALO, rows)], sems.at[1]),
        pltpu.make_async_copy(high, state.at[:, pl.ds(HALO + rows, HALO)], sems.at[2]),
    ]
    for copy in copies:
        copy.start()
    for copy in copies:
        copy.wait()

    lane = lax.broadcasted_iota(jnp.int32, (8, LANES), 1)
    is_first = lane == 0
    is_last = lane == LANES - 1
    chunk_width = centre.shape[3]
    per = chunk_width // LANES

    def begin(i, carry):
        f = i // tiles
        t = i % tiles
        at = pl.ds(pl.multiple_of(t * LANES, LANES), LANES)
        chunk = t // per
        inner = pl.ds(pl.multiple_of((t % per) * LANES, LANES), LANES)
        for r in range(tall):
            if r < HALO:
                base = low_c[chunk, f, pl.ds(low_c.shape[2] - HALO + r, 1), inner]
            elif r < HALO + rows:
                base = centre[chunk, f, pl.ds(r - HALO, 1), inner]
            else:
                base = high_c[chunk, f, pl.ds(r - HALO - rows, 1), inner]
            state[f, r, :, at] = base + perturb * state[f, r, :, at]
        return carry

    lax.fori_loop(0, 3 * tiles, begin, 0)

    def cut(t):
        return pl.ds((t % tiles) * LANES, LANES)

    def shifted(pieces):
        left = [pltpu.roll(p, LANES - 1, 1) for p in pieces]
        right = [pltpu.roll(p, 1, 1) for p in pieces]
        return left, right

    def spread(left, right, t):
        nxt = jnp.where(is_last, left[(t + 1) % tiles], left[t])
        prv = jnp.where(is_first, right[(t - 1) % tiles], right[t])
        return nxt - prv

    def height_row(h, u, v, hn, r):
        flow = [(1.0 + h(r, t)) * v(r, t) for t in range(tiles)]
        left, right = shifted(flow)
        for t in range(tiles):
            below = (1.0 + h(r + 1, t)) * u(r + 1, t)
            above = (1.0 + h(r - 1, t)) * u(r - 1, t)
            hn(r, t, h(r, t) - (0.5 * time_step) * ((below - above) + spread(left, right, t)))

    def momentum_row(h, u, v, un, vn, r):
        hl, hr = shifted([h(r, t) for t in range(tiles)])
        ul, ur = shifted([u(r, t) for t in range(tiles)])
        vl, vr = shifted([v(r, t) for t in range(tiles)])
        for t in range(tiles):
            cu, cv = u(r, t), v(r, t)
            du = (h(r + 1, t) - h(r - 1, t)) + cu * (u(r + 1, t) - u(r - 1, t)) + cv * spread(ul, ur, t)
            dv = spread(hl, hr, t) + cu * (v(r + 1, t) - v(r - 1, t)) + cv * spread(vl, vr, t)
            un(r, t, cu + (time_step * coriolis) * cv - (0.5 * time_step) * du)
            vn(r, t, cv - (time_step * coriolis) * cu - (0.5 * time_step) * dv)

    def reader(ref, *lead):
        return lambda r, t: ref[(*lead, r, slice(None), cut(t))]

    def writer(ref, *lead):
        def put(r, t, value):
            ref[(*lead, r, slice(None), cut(t))] = value

        return put

    h = (state, 0)
    pairs = [((state, 1), (state, 2)), ((spare, 0), (spare, 1))]
    for step in range(STEPS):
        (u, v), (un, vn) = pairs[step % 2], pairs[1 - step % 2]
        low_row = 2 * step + 1
        fresh = (heights, step)

        def height_body(r, carry):
            height_row(reader(*h), reader(*u), reader(*v), writer(*fresh), r)
            return carry

        lax.fori_loop(low_row, tall - low_row, height_body, 0)
        if step + 1 < STEPS:

            def momentum_body(r, carry):
                momentum_row(reader(*fresh), reader(*u), reader(*v), writer(*un), writer(*vn), r)
                return carry

            lax.fori_loop(low_row + 1, tall - low_row - 1, momentum_body, 0)
        h = fresh

    points = obs_weight.shape[0]
    stations = obs_weight.shape[1]
    for group in range(stations // LANES):

        def pick(s, held):
            here = lane == s
            fresh_held = list(held)
            for k in range(points):
                spot = spots[k, group * LANES + s]
                turn = turns[k, group * LANES + s]
                row = spot // tiles
                at = pl.ds(pl.multiple_of((spot % tiles) * LANES, LANES), LANES)
                for step in range(STEPS):
                    value = pltpu.roll(heights[step, HALO + row, :, at], turn, 1)
                    fresh_held[step * points + k] = jnp.where(here, value, held[step * points + k])
            return tuple(fresh_held)

        zero = jnp.zeros((8, LANES), jnp.float32)
        held = lax.fori_loop(0, LANES, pick, (zero,) * (STEPS * points))
        for step in range(STEPS):
            total = None
            for k in range(points):
                term = obs_weight[pl.ds(k, 1), pl.ds(group * LANES, LANES)] * held[step * points + k]
                total = term if total is None else total + term
            out[step, group] = total


def run_model(spots, turns, low_c, centre, high_c, obs_weight, own, low, high):
    fields, rows, members, columns = own.shape
    tall = rows + 2 * HALO
    smem = pl.BlockSpec(memory_space=pltpu.SMEM)
    vmem = pl.BlockSpec(memory_space=pltpu.VMEM)
    raw = pl.BlockSpec(memory_space=pl.ANY)
    groups = obs_weight.shape[1] // LANES
    return pl.pallas_call(
        model_kernel,
        in_specs=[smem, smem, vmem, vmem, vmem, vmem, raw, raw, raw],
        out_specs=vmem,
        out_shape=jax.ShapeDtypeStruct((STEPS, groups, members, LANES), jnp.float32),
        scratch_shapes=[
            pltpu.VMEM((fields, tall, members, columns), jnp.float32),
            pltpu.VMEM((STEPS, tall, members, columns), jnp.float32),
            pltpu.VMEM((2, tall, members, columns), jnp.float32),
            pltpu.SemaphoreType.DMA((3,)),
        ],
        compiler_params=pltpu.CompilerParams(vmem_limit_bytes=56 << 20),
        name="model",
    )(spots, turns, low_c, centre, high_c, obs_weight, own, low, high)


def statistics_kernel(every, own, value, var, anom, packed):
    sources, steps, groups, members, _ = every.shape
    total = sources * members
    gram = jnp.zeros((total, total), jnp.float32)
    pull = jnp.zeros((total, 1), jnp.float32)
    for step in range(steps):
        for group in range(groups):
            at = pl.ds(group * LANES, LANES)
            y = every[:, step, group].reshape(total, LANES)
            mean = jnp.sum(y, axis=0, keepdims=True) * (1.0 / total)
            anom[:, step, at] = (own[step, group] - mean) / perturb
            flat = (y - mean) / perturb
            weighted = flat * (1.0 / var[pl.ds(step, 1), at])
            gram = gram + lax.dot_general(
                weighted,
                flat,
                (((1,), (1,)), ((), ())),
                precision=lax.Precision.HIGHEST,
                preferred_element_type=jnp.float32,
            )
            innov = value[pl.ds(step, 1), at] - mean
            pull = pull + jnp.sum(weighted * innov, axis=1, keepdims=True)
    packed[:, pl.ds(0, total)] = gram
    packed[:, pl.ds(total, LANES - total)] = jnp.broadcast_to(pull, (total, LANES - total))


def statistics(every, own, value, var):
    sources, steps, groups, members, _ = every.shape
    return pl.pallas_call(
        statistics_kernel,
        out_shape=[
            jax.ShapeDtypeStruct((members, steps, groups * LANES), jnp.float32),
            jax.ShapeDtypeStruct((sources * members, LANES), jnp.float32),
        ],
        name="statistics",
    )(every, own, value, var)


def body(
    anomalies,
    mean_state,
    weights,
    station_row,
    station_col,
    stencil_row,
    stencil_col,
    obs_weight,
    obs_value,
    obs_var,
):
    members, fields, rows, columns = anomalies.shape
    total = weights.shape[0]
    place = lax.axis_index("mem")
    chunks = lax.axis_size("mem")
    width = columns // chunks

    col = (station_col[None, :] + stencil_col) % columns
    spots = (station_row[None, :] + stencil_row) * (columns // LANES) + col // LANES
    slot = jnp.arange(col.shape[1], dtype=jnp.int32)[None, :]
    turns = (slot - col) % LANES

    own, top, bottom, partial_sum = prepare(place.reshape(1), weights, anomalies)
    low = lax.ppermute(bottom, "sp", ring("sp", 1))
    high = lax.ppermute(top, "sp", ring("sp", -1))

    pieces = lax.all_to_all(partial_sum, "mem", 0, 0, tiled=True)
    mean_piece = lax.dynamic_slice_in_dim(mean_state, place * width, width, 2)
    centre_piece = mean_piece + jnp.sum(pieces, axis=0)
    centre = lax.all_to_all(
        jnp.broadcast_to(centre_piece[None], (chunks, *centre_piece.shape)), "mem", 0, 0, tiled=True
    )
    edge = 8
    low_c = lax.ppermute(centre[:, :, rows - edge :], "sp", ring("sp", 1))
    high_c = lax.ppermute(centre[:, :, :edge], "sp", ring("sp", -1))

    seen = run_model(spots, turns, low_c, centre, high_c, obs_weight, own, low, high)
    every = lax.all_to_all(jnp.broadcast_to(seen[None], (chunks, *seen.shape)), "mem", 0, 0, tiled=True)
    obs_anom, packed = statistics(every, seen, obs_value, obs_var)
    count = lax.axis_size("sp")
    hop = 1
    while hop < count:
        packed = packed + lax.ppermute(packed, "sp", [(i, i ^ hop) for i in range(count)])
        hop *= 2
    hessian = packed[:, :total] + (total - 1) * jnp.eye(total, dtype=jnp.float32)
    gradient = (total - 1) * weights - packed[:, total]
    return (obs_anom, gradient, hessian)


def solution(mesh):
    return jax.shard_map(
        body,
        mesh=mesh,
        in_specs=(
            P("mem", None, "sp", None),
            P(None, "sp", None),
            P(),
            P("sp"),
            P("sp"),
            P(None, "sp"),
            P(None, "sp"),
            P(None, "sp"),
            P(None, "sp"),
            P(None, "sp"),
        ),
        out_specs=(P("mem", None, "sp"), P(), P()),
        check_vma=False,
    )
```

time: 459 us -> 199 us (0.43); the launches traced: 450 us -> 198 us
  local copies, waits for them, and re-layouts: 139 us -> 5.3 us
  Pallas kernels: 0 us -> 87.3 us
  blocking collectives: 93.4 us -> 28.2 us
  waiting for transfers between devices: 113 us -> 53.8 us
  other arithmetic: 38.2 us -> 4.19 us
  starting transfers between devices: 39.3 us -> 18.7 us
  between operations: 15.1 us -> 0.77 us
  matrix products: 12 us -> 0 us
    pallas_call x0 -> x3, Pallas kernels: none -> 87.3 us  [the longest x1 77.2 us: run_model(): pl.pallas_call(model_kernel, in_specs=[smem, smem, vmem, vmem, vmem, vmem...]
    psum x1 -> x0, waiting for transfers between devices: 78.6 us -> none  [body(): increment = lax.psum(partial_value, 'mem')]
    psum x1 -> x0, blocking collectives: 65 us -> none  [body(): gram, pull = lax.psum((gram, pull), 'sp')]
    sub x4 -> x0, local copies, waits for them, and re-layouts: 63.1 us -> none  [height_update(): height[:, 1:-1]]
    gather x4 -> x0, local copies, waits for them, and re-layouts: 54.6 us -> none  [observe(): picked = jnp.take(flat, flat_index, axis=1)]
    all_to_all x0 -> x1, waiting for transfers between devices: none -> 34.9 us  [body(): pieces = lax.all_to_all(partial_sum, 'mem', 0, 0, tiled=True)]
    all_gather x1 -> x0, blocking collectives: 28.4 us -> none  [body(): gathered = lax.all_gather(own_obs, 'mem', axis=0, tiled=True)]
    all_to_all x0 -> x2, blocking collectives: none -> 28.2 us  [the longest x1 17.8 us: body(): lax.all_to_all(jnp.broadcast_to(centre_piece[None], (chunks, *centre_piec...]
  transfers between devices with their start and end apart: 15 -> 9, of which waited for: 10 -> 6; matrix products, arithmetic and copies ran while one was open for 21% -> 1% of each run, Pallas kernels for 0% -> 0%
where the time goes in v1:
time: 199 us; the launch traced here: 198 us
  Pallas kernels  87.3 us (44%)
  waiting for transfers between devices  53.8 us (27%)
  blocking collectives  28.2 us (14%)
  starting transfers between devices  18.7 us (9%)
  local copies, waits for them, and re-layouts  5.3 us (3%)
  other arithmetic  4.19 us (2%)
    pallas_call x1, Pallas kernels, run_model(): pl.pallas_call(model_kernel, in_specs=[smem, smem, vmem, vmem, vmem, vmem...  77.2 us
    all_to_all x1, waiting for transfers between devices, body(): pieces = lax.all_to_all(partial_sum, 'mem', 0, 0, tiled=True)  34.9 us
    all_to_all x1, blocking collectives, body(): lax.all_to_all(jnp.broadcast_to(centre_piece[None], (chunks, *centre_piec...  17.8 us
    ppermute x4, waiting for transfers between devices, body(): lax.ppermute(packed, 'sp', [(i, i ^ hop) for i in range(count)])  14.1 us
    all_to_all x1, blocking collectives, body(): lax.all_to_all(jnp.broadcast_to(seen[None], (chunks, *seen.shape)), 'mem'...  10.4 us
    pallas_call x1, Pallas kernels, prepare(): pl.pallas_call(prepare_kernel, grid=(fields, 2), in_specs=[smem, smem, pl...  7.92 us
    all_to_all x1, starting transfers between devices, body(): pieces = lax.all_to_all(partial_sum, 'mem', 0, 0, tiled=True)  5.67 us
    ppermute x1, starting transfers between devices, body(): high = lax.ppermute(top, 'sp', ring('sp', -1))  5.59 us
  transfers between devices with their start and end apart: 9, of which 6 were waited for; matrix products, arithmetic and copies ran while one was open for 1% of the time, Pallas kernels for 0%

profile of v1, /device:TPU:0, one launch (start us, length us, event | category | flops | bytes accessed | tf_op | source)
XLA Modules:
  0.0 198.2 jit_solution(17632803076929604855)
XLA Ops:
  0.6 0.0 copy-start.1
  0.6 0.6 copy-done.1
  1.3 7.9 %prepare.1 = (f32[3,16,8,4096]{3,2,1,0:T(8,128)S(1)}, f32[3,7,8,4096]{3,2,1,0:T(8,128)S(1)}, f32[3,7,8,4096]{3,2,1,0:T(8,128)}, f32[8,3,16,512]{3,2,1,0:T(8,128)}) custom-call(s32[1]{0:T(128)} %bitcast.place, f32[64]{0:T(128)S(1)} %copy-done.1, f32[8,3,16,4096]{3,2,1,0:T(8,128)} %anom.1), custom_call_target="tpu_custom_call" | custom-call | tf_op jit(solution)/shard_map/prepare/pallas_call | solution.py:58
  9.2 2.7 %copy-done = f32[3,16,8,4096]{3,2,1,0:T(8,128)} copy-done((f32[3,16,8,4096]{3,2,1,0:T(8,128)}, f32[3,16,8,4096]{3,2,1,0:T(8,128)S(1)}, u32[]{:S(2)}) %copy-start) | copy-done | bytes 6291480
  11.9 5.6 %collective-permute-start.3 = (f32[3,7,8,4096]{3,2,1,0:T(8,128)S(1)}, f32[3,7,8,4096]{3,2,1,0:T(8,128)}, u32[]{:S(2)}, u32[]{:S(2)}) collective-permute-start(f32[3,7,8,4096]{3,2,1,0:T(8,128)S(1)} %get-tuple-element.12), channel_id=1, source_target_pairs={{0,15},{1,0},{2,1},{3,2},{4,3},{5,4},{6,5},{7,6},{8,7},{9,8},{10,9... | collective-permute-start | bytes 8257544 | tf_op jit(solution)/shard_map/ppermute | solution.py:294
  17.5 5.7 %all-to-all-start = ((f32[8,3,16,512]{3,2,1,0:T(8,128)}), f32[8,3,16,512]{3,2,1,0:T(8,128)S(1)}, u32[]{:S(2)}, u32[]{:S(2)}) async-start(f32[8,3,16,512]{3,2,1,0:T(8,128)} %get-tuple-element.9), calls=%async_computation | async-start | bytes 1572864 | tf_op jit(solution)/shard_map/all_to_all | solution.py:296
  23.2 34.9 %all-to-all-done = f32[8,3,16,512]{3,2,1,0:T(8,128)S(1)} async-done(((f32[8,3,16,512]{3,2,1,0:T(8,128)}), f32[8,3,16,512]{3,2,1,0:T(8,128)S(1)}, u32[]{:S(2)}, u32[]{:S(2)}) %all-to-all-start) | async-done | bytes 786464 | tf_op jit(solution)/shard_map/all_to_all | solution.py:296
  58.1 0.7 reduce_sum.9
  58.8 1.0 dynamic-slice_add_fusion
  59.7 0.1 broadcast_in_dim.4
  59.8 17.8 %all_to_all.15.centre = f32[8,3,16,512]{3,2,1,0:T(8,128)S(1)} all-to-all(f32[8,3,16,512]{3,2,1,0:T(8,128)S(1)} %broadcast_in_dim.4), channel_id=1, replica_groups=mesh['mem'=8,'sp'=16] {'mem'}, dimensions={0} | all-to-all | bytes 1572864 | tf_op jit(solution)/shard_map/all_to_all | solution.py:299
  77.6 0.1 fusion.5
  77.6 0.1 collective-permute-start
  77.7 5.3 %collective-permute-start.1 = (f32[8,3,8,512]{3,2,1,0:T(8,128)S(1)}, f32[8,3,8,512]{3,2,1,0:T(8,128)S(1)}, u32[]{:S(2)}, u32[]{:S(2)}) collective-permute-start(f32[8,3,8,512]{3,2,1,0:T(8,128)S(1)} %get-tuple-element.15), channel_id=1, source_target_pairs={{0,15},{1,0},{2,1},{3,2},{4,3},{5,4},{6,5},{7,6},{8,7},{9,8},{10,9... | collective-permute-start | bytes 1179656 | tf_op jit(solution)/shard_map/ppermute | solution.py:304
  83.1 0.6 add_select_fusion
  83.7 4.8 %collective-permute-done.low_c = f32[8,3,8,512]{3,2,1,0:T(8,128)S(1)} collective-permute-done((f32[8,3,8,512]{3,2,1,0:T(8,128)S(1)}, f32[8,3,8,512]{3,2,1,0:T(8,128)S(1)}, u32[]{:S(2)}, u32[]{:S(2)}) %collective-permute-start) | collective-permute-done | bytes 393248 | tf_op jit(solution)/shard_map/ppermute | solution.py:303
  88.6 0.7 copy-done.4
  89.3 0.1 copy-done.5
  89.4 77.2 %model.1.own = f32[4,2,8,128]{3,2,1,0:T(8,128)} custom-call(s32[4,256]{1,0:T(4,128)} %get-tuple-element.18.spots, s32[4,256]{1,0:T(4,128)} %get-tuple-element.17.turns, f32[8,3,8,512]{3,2,1,0:T(8,128)} %copy-done.4, f32[8,3,16,512]{3,2,1,0:T(8,128)} %copy-done.3, f32[8,3,8,512]{3,2,1,0:T(8,128)} %copy-done.5, f32[4,256]{1,0:T(4,128)} %obs_weight.1, ...), custom_call_target="tpu_custom_call" | custom-call | tf_op jit(solution)/shard_map/model/pallas_call | solution.py:215
  166.6 0.8 broadcast_in_dim.5
  167.4 10.4 %all_to_all.16.every = f32[8,4,2,8,128]{4,3,2,1,0:T(8,128)} all-to-all(f32[8,4,2,8,128]{4,3,2,1,0:T(8,128)S(1)} %broadcast_in_dim.5), channel_id=1, replica_groups=mesh['mem'=8,'sp'=16] {'mem'}, dimensions={0} | all-to-all | bytes 524288 | tf_op jit(solution)/shard_map/all_to_all | solution.py:307
  177.8 2.2 %statistics.1 = (f32[8,4,256]{2,1,0:T(4,128)}, f32[64,128]{1,0:T(8,128)}) custom-call(f32[8,4,2,8,128]{4,3,2,1,0:T(8,128)} %all_to_all.16.every, f32[4,2,8,128]{3,2,1,0:T(8,128)} %model.1.own, f32[4,256]{1,0:T(4,128)} %value.1, f32[4,256]{1,0:T(4,128)} %var.1), custom_call_target="tpu_custom_call" | custom-call | tf_op jit(solution)/shard_map/statistics/pallas_call | solution.py:259
  179.9 1.4 collective-permute-done.4
  181.4 0.8 add.60
  182.1 3.9 %collective-permute-done.5 = f32[64,128]{1,0:T(8,128)S(1)} collective-permute-done((f32[64,128]{1,0:T(8,128)S(1)}, f32[64,128]{1,0:T(8,128)S(1)}, u32[]{:S(2)}, u32[]{:S(2)}) %collective-permute-start.5) | collective-permute-done | bytes 32800 | tf_op jit(solution)/shard_map/ppermute | solution.py:312
  186.1 1.3 collective-permute-start.6
  187.4 4.1 %collective-permute-done.6 = f32[64,128]{1,0:T(8,128)S(1)} collective-permute-done((f32[64,128]{1,0:T(8,128)S(1)}, f32[64,128]{1,0:T(8,128)S(1)}, u32[]{:S(2)}, u32[]{:S(2)}) %collective-permute-start.6) | collective-permute-done | bytes 32800 | tf_op jit(solution)/shard_map/ppermute | solution.py:312
  191.5 0.7 collective-permute-start.7
  192.2 4.7 %collective-permute-done.7 = f32[64,128]{1,0:T(8,128)S(1)} collective-permute-done((f32[64,128]{1,0:T(8,128)S(1)}, f32[64,128]{1,0:T(8,128)S(1)}, u32[]{:S(2)}, u32[]{:S(2)}) %collective-permute-start.7) | collective-permute-done | bytes 32800 | tf_op jit(solution)/shard_map/ppermute | solution.py:312
  196.9 0.6 slice_add_fusion
  197.5 0.2 slice_reduce_fusion
  197.7 0.5 multiply_subtract_fusion
  (24 shorter events, 0.1 us)
Async XLA Ops:
  0.6 0.7 copy-start.1
  9.2 2.7 %copy-start = (f32[3,16,8,4096]{3,2,1,0:T(8,128)}, f32[3,16,8,4096]{3,2,1,0:T(8,128)S(1)}, u32[]{:S(2)}) copy-start(f32[3,16,8,4096]{3,2,1,0:T(8,128)S(1)} %get-tuple-element.10.own) | copy-start | bytes 18874372
  11.9 76.7 %collective-permute-start.2 = (f32[3,7,8,4096]{3,2,1,0:T(8,128)}, f32[3,7,8,4096]{3,2,1,0:T(8,128)}, u32[]{:S(2)}, u32[]{:S(2)}) collective-permute-start(f32[3,7,8,4096]{3,2,1,0:T(8,128)} %get-tuple-element.11), channel_id=1, source_target_pairs={{0,1},{1,2},{2,3},{3,4},{4,5},{5,6},{6,7},{7,8},{8,9},{9,10},{10,1... | collective-permute-start | bytes 8257544 | tf_op jit(solution)/shard_map/ppermute | solution.py:293
  11.9 76.7 %collective-permute-start.3 = (f32[3,7,8,4096]{3,2,1,0:T(8,128)S(1)}, f32[3,7,8,4096]{3,2,1,0:T(8,128)}, u32[]{:S(2)}, u32[]{:S(2)}) collective-permute-start(f32[3,7,8,4096]{3,2,1,0:T(8,128)S(1)} %get-tuple-element.12), channel_id=1, source_target_pairs={{0,15},{1,0},{2,1},{3,2},{4,3},{5,4},{6,5},{7,6},{8,7},{9,8},{10,9... | collective-permute-start | bytes 8257544 | tf_op jit(solution)/shard_map/ppermute | solution.py:294
  17.5 40.6 %all-to-all-start = ((f32[8,3,16,512]{3,2,1,0:T(8,128)}), f32[8,3,16,512]{3,2,1,0:T(8,128)S(1)}, u32[]{:S(2)}, u32[]{:S(2)}) async-start(f32[8,3,16,512]{3,2,1,0:T(8,128)} %get-tuple-element.9), calls=%async_computation | async-start | bytes 1572864 | tf_op jit(solution)/shard_map/all_to_all | solution.py:296
  23.1 59.9 %copy-start.6 = (s32[4,256]{1,0:T(4,128)S(1)}, s32[4,256]{1,0:T(4,128)}, u32[]{:S(2)}) copy-start(s32[4,256]{1,0:T(4,128)} %param.16) | copy-start | bytes 12292
  23.1 59.9 %copy-start.7 = (s32[4,256]{1,0:T(4,128)S(1)}, s32[4,256]{1,0:T(4,128)}, u32[]{:S(2)}) copy-start(s32[4,256]{1,0:T(4,128)} %param.15) | copy-start | bytes 12292
  23.2 59.9 %copy-start.8 = (s32[256]{0:T(256)S(1)}, s32[256]{0:T(256)}, u32[]{:S(2)}) copy-start(s32[256]{0:T(256)} %param.14) | copy-start | bytes 3076
  23.2 59.9 %copy-start.9 = (s32[256]{0:T(256)S(1)}, s32[256]{0:T(256)}, u32[]{:S(2)}) copy-start(s32[256]{0:T(256)} %param.13) | copy-start | bytes 3076
  77.6 11.0 %copy-start.3 = (f32[8,3,16,512]{3,2,1,0:T(8,128)}, f32[8,3,16,512]{3,2,1,0:T(8,128)S(1)}, u32[]{:S(2)}) copy-start(f32[8,3,16,512]{3,2,1,0:T(8,128)S(1)} %all_to_all.15.centre) | copy-start | bytes 2359300
  77.6 10.9 %collective-permute-start = (f32[8,3,8,512]{3,2,1,0:T(8,128)S(1)}, f32[8,3,8,512]{3,2,1,0:T(8,128)S(1)}, u32[]{:S(2)}, u32[]{:S(2)}) collective-permute-start(f32[8,3,8,512]{3,2,1,0:T(8,128)S(1)} %get-tuple-element.16), channel_id=1, source_target_pairs={{0,1},{1,2},{2,3},{3,4},{4,5},{5,6},{6,7},{7,8},{8,9},{9,10},{10,1... | collective-permute-start | bytes 1179656 | tf_op jit(solution)/shard_map/ppermute | solution.py:303
  77.7 10.8 %collective-permute-start.1 = (f32[8,3,8,512]{3,2,1,0:T(8,128)S(1)}, f32[8,3,8,512]{3,2,1,0:T(8,128)S(1)}, u32[]{:S(2)}, u32[]{:S(2)}) collective-permute-start(f32[8,3,8,512]{3,2,1,0:T(8,128)S(1)} %get-tuple-element.15), channel_id=1, source_target_pairs={{0,15},{1,0},{2,1},{3,2},{4,3},{5,4},{6,5},{7,6},{8,7},{9,8},{10,9... | collective-permute-start | bytes 1179656 | tf_op jit(solution)/shard_map/ppermute | solution.py:304
  88.5 0.8 copy-start.4
  88.5 0.9 copy-start.5
  89.4 108.3 %copy-start.2 = (f32[64]{0:T(128)S(1)}, f32[64]{0:T(128)}, u32[]{:S(2)}) copy-start(f32[64]{0:T(128)} %weights.1) | copy-start | bytes 772
  179.9 1.4 collective-permute-start.4
  182.1 3.9 %collective-permute-start.5 = (f32[64,128]{1,0:T(8,128)S(1)}, f32[64,128]{1,0:T(8,128)S(1)}, u32[]{:S(2)}, u32[]{:S(2)}) collective-permute-start(f32[64,128]{1,0:T(8,128)S(1)} %add.60), channel_id=1, source_target_pairs={{0,2},{1,3},{2,0},{3,1},{4,6},{5,7},{6,4},{7,5},{8,10},{9,11},{10,... | collective-permute-start | bytes 98312 | tf_op jit(solution)/shard_map/ppermute | solution.py:312
  186.1 5.4 %collective-permute-start.6 = (f32[64,128]{1,0:T(8,128)S(1)}, f32[64,128]{1,0:T(8,128)S(1)}, u32[]{:S(2)}, u32[]{:S(2)}) collective-permute-start(f32[64,128]{1,0:T(8,128)S(1)} %add.61), channel_id=1, source_target_pairs={{0,4},{1,5},{2,6},{3,7},{4,0},{5,1},{6,2},{7,3},{8,12},{9,13},{10,... | collective-permute-start | bytes 98312 | tf_op jit(solution)/shard_map/ppermute | solution.py:312
  191.5 5.4 %collective-permute-start.7 = (f32[64,128]{1,0:T(8,128)S(1)}, f32[64,128]{1,0:T(8,128)S(1)}, u32[]{:S(2)}, u32[]{:S(2)}) collective-permute-start(f32[64,128]{1,0:T(8,128)S(1)} %add.62), channel_id=1, source_target_pairs={{0,8},{1,9},{2,10},{3,11},{4,12},{5,13},{6,14},{7,15},{8,0},{9,1},... | collective-permute-start | bytes 98312 | tf_op jit(solution)/shard_map/ppermute | solution.py:312

commit v2 on v1

v2 whole, which is shorter than its diff:
```python
import jax
import jax.numpy as jnp
from jax import lax
from jax.experimental import pallas as pl
from jax.experimental.pallas import tpu as pltpu
from jax.sharding import PartitionSpec as P

STEPS = 4
HALO = 2 * STEPS - 1
EARLY = 3
LANES = 128
GROUP = 4
PAIR = 2
SPAN = 4
NEAR = 4
VMEM_MODEL = 38 << 20
ROWS = 2

time_step = 1.0
coriolis = 0.1
perturb = 0.1


def in_hbm(array):
    return pltpu.with_memory_space_constraint(array, pltpu.HBM)


def ring(axis, step):
    count = lax.axis_size(axis)
    return [(i, (i + step) % count) for i in range(count)]


def prepare_kernel(place, weights, anom, turned, top, top_more, bottom, bottom_more, partial):
    members, rows = anom.shape[0], anom.shape[2]
    chunks, width = partial.shape[0], partial.shape[3]
    first = place[0] * members
    scales = [weights[first + m] for m in range(members)]

    per = width // (SPAN * LANES)

    def columns(c, carry):
        swapped, totals = [], []
        for i in range(SPAN):
            block = anom[:, 0, :, pl.ds(pl.multiple_of((c * SPAN + i) * LANES, LANES), LANES)]
            swapped.append(jnp.swapaxes(block, 0, 1))
            total = scales[0] * block[0]
            for m in range(1, members):
                total = total + scales[m] * block[m]
            totals.append(total)
        inner = pl.multiple_of(lax.rem(c, per) * (SPAN * LANES), SPAN * LANES)
        for i in range(SPAN):
            turned[0, :, c * SPAN + i] = swapped[i]
            partial[lax.div(c, per), 0, :, pl.ds(inner + i * LANES, LANES)] = totals[i]
        return carry

    lax.fori_loop(0, chunks * per, columns, 0)

    @pl.when(pl.program_id(1) == 0)
    def _():
        top[0] = turned[0, :EARLY]
        top_more[0] = turned[0, EARLY:HALO]

    @pl.when(pl.program_id(1) == 1)
    def _():
        bottom[0] = turned[0, rows - HALO : rows - HALO + EARLY]
        bottom_more[0] = turned[0, rows - HALO + EARLY :]


def prepare(place, weights, anomalies):
    members, fields, rows, columns = anomalies.shape
    half = rows // 2
    chunks = NEAR
    width = columns // chunks
    smem = pl.BlockSpec(memory_space=pltpu.SMEM)
    tiles = columns // LANES
    parts = (EARLY, HALO - EARLY) * 2
    return pl.pallas_call(
        prepare_kernel,
        grid=(fields, 2),
        in_specs=[smem, smem, pl.BlockSpec((members, 1, half, columns), lambda f, r: (0, f, r, 0))],
        out_specs=[
            pl.BlockSpec((1, half, tiles, members, LANES), lambda f, r: (f, r, 0, 0, 0)),
            *(pl.BlockSpec((1, part, tiles, members, LANES), lambda f, r: (f, 0, 0, 0, 0)) for part in parts),
            pl.BlockSpec((chunks, 1, half, width), lambda f, r: (0, f, r, 0)),
        ],
        out_shape=[
            pltpu.HBM((fields, rows, tiles, members, LANES), jnp.float32),
            *(pltpu.HBM((fields, part, tiles, members, LANES), jnp.float32) for part in parts),
            jax.ShapeDtypeStruct((chunks, fields, rows, width), jnp.float32),
        ],
        compiler_params=pltpu.CompilerParams(vmem_limit_bytes=40 << 20),
        name="prepare",
    )(place, weights, anomalies)


def model_kernel(
    spots, turns, low_c, centre, high_c, obs_weight, own, low, low_more, high, high_more, out, state, heights, spare, sems
):
    rows, tiles = own.shape[1], own.shape[2]
    tall = rows + 2 * HALO
    copies = []
    row = 0
    for source in (low, low_more, own, high, high_more):
        part = source.shape[1]
        for f in range(3):
            target = state.at[f, pl.ds(row, part)]
            copies.append(pltpu.make_async_copy(source.at[f], target, sems.at[len(copies)]))
        row += part
    for copy in copies:
        copy.start()
    for copy in copies:
        copy.wait()

    lane = lax.broadcasted_iota(jnp.int32, (8, LANES), 1)
    is_first = lane == 0
    is_last = lane == LANES - 1
    chunk_width = centre.shape[3]
    per = chunk_width // LANES

    edge = low_c.shape[2]

    def begin(i, carry):
        f = lax.div(i, tiles // PAIR)
        first = lax.rem(i, tiles // PAIR) * PAIR
        chunk = lax.div(first, per)
        inner = pl.multiple_of(lax.rem(first, per) * LANES, PAIR * LANES)
        for base, skip, at, count in (
            (low_c, edge - HALO, 0, HALO),
            (centre, 0, HALO, rows),
            (high_c, 0, HALO + rows, HALO),
        ):
            ready = []
            for r in range(count):
                for t in range(PAIR):
                    middle = base[chunk, f, pl.ds(skip + r, 1), pl.ds(inner + t * LANES, LANES)]
                    ready.append((r, t, middle + perturb * state[f, at + r, first + t]))
            for r, t, value in ready:
                state[f, at + r, first + t] = value
        return carry

    lax.fori_loop(0, 3 * tiles // PAIR, begin, 0)

    def memo(fetch):
        kept = {}

        def get(t):
            if isinstance(t, int):
                t %= tiles
            if t not in kept:
                kept[t] = fetch(t)
            return kept[t]

        return get

    def slope(piece):
        left = memo(lambda t: pltpu.roll(piece(t), LANES - 1, 1))
        right = memo(lambda t: pltpu.roll(piece(t), 1, 1))
        return lambda t: jnp.where(is_last, left(t + 1), left(t)) - jnp.where(is_first, right(t - 1), right(t))

    def rows_of(field, r):
        return memo(lambda key: field(r + key[0], key[1] % tiles))

    def in_row(get, i):
        return memo(lambda t: get((i, t)))

    def sweep(make, puts, r):
        for start in range(0, tiles, GROUP):
            span = range(start, start + GROUP)
            ready = [[make[i](t) for t in span] for i in range(len(make))]
            for i, values in enumerate(ready):
                for t, value in zip(span, values):
                    for put, part in zip(puts, value):
                        put(r + i, t, part)

    def height_rows(h, u, v, hn, r):
        gh, gu = rows_of(h, r), rows_of(u, r)
        flow = memo(lambda key: (1.0 + gh(key)) * gu(key))

        def row(i):
            across = slope(memo(lambda t: (1.0 + gh((i, t))) * v(r + i, t)))

            def value(t):
                along = flow((i + 1, t)) - flow((i - 1, t))
                return (gh((i, t)) - (0.5 * time_step) * (along + across(t)),)

            return value

        sweep([row(i) for i in range(ROWS)], (hn,), r)

    def momentum_rows(h, u, v, un, vn, r):
        gh, gu, gv = rows_of(h, r), rows_of(u, r), rows_of(v, r)

        def row(i):
            slope_h, slope_u, slope_v = slope(in_row(gh, i)), slope(in_row(gu, i)), slope(in_row(gv, i))

            def value(t):
                cu, cv = gu((i, t)), gv((i, t))
                du = (gh((i + 1, t)) - gh((i - 1, t))) + cu * (gu((i + 1, t)) - gu((i - 1, t))) + cv * slope_u(t)
                dv = slope_h(t) + cu * (gv((i + 1, t)) - gv((i - 1, t))) + cv * slope_v(t)
                return (
                    cu + (time_step * coriolis) * cv - (0.5 * time_step) * du,
                    cv - (time_step * coriolis) * cu - (0.5 * time_step) * dv,
                )

            return value

        sweep([row(i) for i in range(ROWS)], (un, vn), r)

    def reader(ref, *lead):
        return lambda r, t: ref[(*lead, r, t)]

    def writer(ref, *lead):
        def put(r, t, value):
            ref[(*lead, r, t)] = value

        return put

    h = (state, 0)
    pairs = [((state, 1), (state, 2)), ((spare, 0), (spare, 1))]
    for step in range(STEPS):
        (u, v), (un, vn) = pairs[step % 2], pairs[1 - step % 2]
        low_row = 2 * step + 1
        fresh = (heights, step)

        def height_body(i, carry):
            height_rows(reader(*h), reader(*u), reader(*v), writer(*fresh), low_row + ROWS * i)
            return carry

        lax.fori_loop(0, (tall - 2 * low_row) // ROWS, height_body, 0)
        if step + 1 < STEPS:

            def momentum_body(i, carry):
                momentum_rows(reader(*fresh), reader(*u), reader(*v), writer(*un), writer(*vn), low_row + 1 + ROWS * i)
                return carry

            lax.fori_loop(0, (tall - 2 * low_row - 2) // ROWS, momentum_body, 0)
        h = fresh

    points = obs_weight.shape[0]
    stations = obs_weight.shape[1]
    for group in range(stations // LANES):

        def pick(s, held):
            here = lane == s
            fresh_held = list(held)
            for k in range(points):
                spot = spots[k, group * LANES + s]
                turn = turns[k, group * LANES + s]
                for step in range(STEPS):
                    value = pltpu.roll(heights[step, HALO + lax.shift_right_logical(spot, tiles.bit_length() - 1), spot & (tiles - 1)], turn, 1)
                    fresh_held[step * points + k] = jnp.where(here, value, held[step * points + k])
            return tuple(fresh_held)

        zero = jnp.zeros((8, LANES), jnp.float32)
        held = lax.fori_loop(0, LANES, pick, (zero,) * (STEPS * points), unroll=16)
        for step in range(STEPS):
            total = None
            for k in range(points):
                term = obs_weight[pl.ds(k, 1), pl.ds(group * LANES, LANES)] * held[step * points + k]
                total = term if total is None else total + term
            out[step, group] = total


def run_model(spots, turns, low_c, centre, high_c, obs_weight, own, *halos):
    fields, rows, tiles, members, _ = own.shape
    tall = rows + 2 * HALO
    smem = pl.BlockSpec(memory_space=pltpu.SMEM)
    vmem = pl.BlockSpec(memory_space=pltpu.VMEM)
    groups = obs_weight.shape[1] // LANES
    return pl.pallas_call(
        model_kernel,
        in_specs=[smem, smem] + [vmem] * 4 + [pl.BlockSpec(memory_space=pltpu.HBM)] * 5,
        out_specs=vmem,
        out_shape=jax.ShapeDtypeStruct((STEPS, groups, members, LANES), jnp.float32),
        scratch_shapes=[
            pltpu.VMEM((fields, tall, tiles, members, LANES), jnp.float32),
            pltpu.VMEM((STEPS, tall, tiles, members, LANES), jnp.float32),
            pltpu.VMEM((2, tall, tiles, members, LANES), jnp.float32),
            pltpu.SemaphoreType.DMA((15,)),
        ],
        compiler_params=pltpu.CompilerParams(vmem_limit_bytes=VMEM_MODEL),
        name="model",
    )(spots, turns, low_c, centre, high_c, obs_weight, own, *halos)


def statistics_kernel(every, own, value, var, anom, packed):
    sources, steps, groups, members, _ = every.shape
    total = sources * members
    gram = jnp.zeros((total, total), jnp.float32)
    pull = jnp.zeros((total, 1), jnp.float32)
    for step in range(steps):
        for group in range(groups):
            at = pl.ds(group * LANES, LANES)
            y = every[:, step, group].reshape(total, LANES)
            mean = jnp.sum(y, axis=0, keepdims=True) * (1.0 / total)
            anom[:, step, at] = (own[step, group] - mean) / perturb
            flat = (y - mean) / perturb
            weighted = flat * (1.0 / var[pl.ds(step, 1), at])
            gram = gram + lax.dot_general(
                weighted,
                flat,
                (((1,), (1,)), ((), ())),
                precision=lax.Precision.HIGHEST,
                preferred_element_type=jnp.float32,
            )
            innov = value[pl.ds(step, 1), at] - mean
            pull = pull + jnp.sum(weighted * innov, axis=1, keepdims=True)
    packed[:, pl.ds(0, total)] = gram
    packed[:, pl.ds(total, LANES - total)] = jnp.broadcast_to(pull, (total, LANES - total))


def statistics(every, own, value, var):
    sources, steps, groups, members, _ = every.shape
    return pl.pallas_call(
        statistics_kernel,
        out_shape=[
            jax.ShapeDtypeStruct((members, steps, groups * LANES), jnp.float32),
            jax.ShapeDtypeStruct((sources * members, LANES), jnp.float32),
        ],
        name="statistics",
    )(every, own, value, var)


def body(
    anomalies,
    mean_state,
    weights,
    station_row,
    station_col,
    stencil_row,
    stencil_col,
    obs_weight,
    obs_value,
    obs_var,
):
    members, fields, rows, columns = anomalies.shape
    total = weights.shape[0]
    place = lax.axis_index("mem")
    count = lax.axis_size("mem")
    near = [[start + i for i in range(NEAR)] for start in range(0, count, NEAR)]
    width = columns // NEAR

    col = (station_col[None, :] + stencil_col) % columns
    spots = (station_row[None, :] + stencil_row) * (columns // LANES) + col // LANES
    slot = jnp.arange(col.shape[1], dtype=jnp.int32)[None, :]
    turns = (slot - col) % LANES

    own, top, top_more, bottom, bottom_more, partial_sum = prepare(place.reshape(1), weights, in_hbm(anomalies))
    low = lax.ppermute(bottom, "sp", ring("sp", 1))
    high = lax.ppermute(top, "sp", ring("sp", -1))

    pieces = lax.all_to_all(partial_sum, "mem", 0, 0, axis_index_groups=near, tiled=True)
    piece = jnp.sum(pieces, axis=0)
    piece, low, high = lax.optimization_barrier((piece, low, high))
    hop = NEAR
    while hop < count:
        piece = piece + lax.ppermute(piece, "mem", [(i, i ^ hop) for i in range(count)])
        hop *= 2
    piece, top_more, bottom_more = lax.optimization_barrier((piece, top_more, bottom_more))
    low_more = lax.ppermute(bottom_more, "sp", ring("sp", 1))
    high_more = lax.ppermute(top_more, "sp", ring("sp", -1))
    piece = piece + lax.dynamic_slice_in_dim(mean_state, lax.rem(place, NEAR) * width, width, 2)
    centre = lax.all_to_all(
        jnp.broadcast_to(piece[None], (NEAR, *piece.shape)), "mem", 0, 0, axis_index_groups=near, tiled=True
    )
    edge = 8
    low_c = lax.ppermute(centre[:, :, rows - edge :], "sp", ring("sp", 1))
    high_c = lax.ppermute(centre[:, :, :edge], "sp", ring("sp", -1))

    seen = run_model(spots, turns, low_c, centre, high_c, obs_weight, *map(in_hbm, (own, low, low_more, high, high_more)))
    every = lax.all_to_all(jnp.broadcast_to(seen[None], (count, *seen.shape)), "mem", 0, 0, tiled=True)
    obs_anom, packed = statistics(every, seen, obs_value, obs_var)
    count = lax.axis_size("sp")
    hop = 1
    while hop < count:
        packed = packed + lax.ppermute(packed, "sp", [(i, i ^ hop) for i in range(count)])
        hop *= 2
    hessian = packed[:, :total] + (total - 1) * jnp.eye(total, dtype=jnp.float32)
    gradient = (total - 1) * weights - packed[:, total]
    return (obs_anom, gradient, hessian)


def solution(mesh):
    return jax.shard_map(
        body,
        mesh=mesh,
        in_specs=(
            P("mem", None, "sp", None),
            P(None, "sp", None),
            P(),
            P("sp"),
            P("sp"),
            P(None, "sp"),
            P(None, "sp"),
            P(None, "sp"),
            P(None, "sp"),
            P(None, "sp"),
        ),
        out_specs=(P("mem", None, "sp"), P(), P()),
        check_vma=False,
    )
```

time: 199 us -> 140 us (0.70)
  Pallas kernels: 87.3 us -> 49 us
  waiting for transfers between devices: 53.8 us -> 19.1 us
  blocking collectives: 28.2 us -> 38.1 us
  starting transfers between devices: 18.7 us -> 25.8 us
  local copies, waits for them, and re-layouts: 5.3 us -> 2.67 us
    pallas_call x1, Pallas kernels: 77.2 us -> 37.7 us  [run_model(): pl.pallas_call(model_kernel, in_specs=[smem, smem] + [vmem] * 4 + [pl.Blo...]
    all_to_all x1 -> x0, waiting for transfers between devices: 34.9 us -> none  [body(): pieces = lax.all_to_all(partial_sum, 'mem', 0, 0, tiled=True)]
    all_to_all x2 -> x3, blocking collectives: 28.2 us -> 38.1 us  [the longest x1 13.9 us: body(): lax.all_to_all(jnp.broadcast_to(piece[None], (NEAR, *piece.shape)), 'mem'...]
    ppermute x0 -> x3, starting transfers between devices: none -> 7.62 us  [the longest x1 5.71 us: body(): high_more = lax.ppermute(top_more, 'sp', ring('sp', -1))]
    all_to_all x1 -> x0, starting transfers between devices: 5.67 us -> none  [body(): pieces = lax.all_to_all(partial_sum, 'mem', 0, 0, tiled=True)]
    ppermute x4, starting transfers between devices: 2.04 us -> 7.14 us  [body(): lax.ppermute(packed, 'sp', [(i, i ^ hop) for i in range(count)])]
    ppermute x4, waiting for transfers between devices: 14.1 us -> 9.49 us  [body(): lax.ppermute(packed, 'sp', [(i, i ^ hop) for i in range(count)])]
    ppermute x0 -> x3, waiting for transfers between devices: none -> 3.91 us  [the longest x1 3.91 us: body(): lax.ppermute(piece, 'mem', [(i, i ^ hop) for i in range(count)])]
  transfers between devices with their start and end apart: 9 -> 11, of which waited for: 6 -> 7; matrix products, arithmetic and copies ran while one was open for 1% -> 1% of each run, Pallas kernels for 0% -> 0%
where the time goes in v2:
time: 140 us; the launch traced here: 138 us
  Pallas kernels  49 us (35%)
  blocking collectives  38.1 us (27%)
  starting transfers between devices  25.8 us (18%)
  waiting for transfers between devices  19.1 us (14%)
  other arithmetic  2.96 us (2%)
  local copies, waits for them, and re-layouts  2.67 us (2%)
    pallas_call x1, Pallas kernels, run_model(): pl.pallas_call(model_kernel, in_specs=[smem, smem] + [vmem] * 4 + [pl.Blo...  37.7 us
    all_to_all x1, blocking collectives, body(): lax.all_to_all(jnp.broadcast_to(piece[None], (NEAR, *piece.shape)), 'mem'...  13.9 us
    all_to_all x1, blocking collectives, body(): lax.all_to_all(partial_sum, 'mem', 0, 0, axis_index_groups=near, tiled=True)  13.7 us
    all_to_all x1, blocking collectives, body(): lax.all_to_all(jnp.broadcast_to(seen[None], (count, *seen.shape)), 'mem',...  10.5 us
    ppermute x4, waiting for transfers between devices, body(): lax.ppermute(packed, 'sp', [(i, i ^ hop) for i in range(count)])  9.49 us
    pallas_call x1, Pallas kernels, prepare(): pl.pallas_call(prepare_kernel, grid=(fields, 2), in_specs=[smem, smem, pl...  9.16 us
    ppermute x4, starting transfers between devices, body(): lax.ppermute(packed, 'sp', [(i, i ^ hop) for i in range(count)])  7.14 us
    ppermute x1, starting transfers between devices, body(): high_more = lax.ppermute(top_more, 'sp', ring('sp', -1))  5.71 us
  transfers between devices with their start and end apart: 11, of which 7 were waited for; matrix products, arithmetic and copies ran while one was open for 1% of the time, Pallas kernels for 0%

profile of v2, /device:TPU:0, one launch (start us, length us, event | category | flops | bytes accessed | tf_op | source)
XLA Modules:
  0.0 138.4 jit_solution(4197080570762837629)
XLA Ops:
  0.6 0.0 copy-start.2
  0.6 0.6 copy-done.2
  1.3 9.2 %prepare.1 = (f32[3,16,32,8,128]{4,3,2,1,0:T(8,128)}, f32[3,3,32,8,128]{4,3,2,1,0:T(8,128)}, f32[3,4,32,8,128]{4,3,2,1,0:T(8,128)}, f32[3,3,32,8,128]{4,3,2,1,0:...) custom-call(s32[1]{0:T(128)} %bitcast.place, f32[64]{0:T(128)S(1)} %copy-done.2, ...), custom_call_target="tpu_custom_call" | custom-call | tf_op jit(solution)/shard_map/prepare/pallas_call | solution.py:77
  10.5 5.6 %collective-permute-start.1 = (f32[3,3,32,8,128]{4,3,2,1,0:T(8,128)}, f32[3,3,32,8,128]{4,3,2,1,0:T(8,128)S(1)}, u32[]{:S(2)}, u32[]{:S(2)}) collective-permute-start(f32[3,3,32,8,128]{4,3,2,1,0:T(8,128)} %get-tuple-element.19), channel_id=1, source_target_pairs={{0,15},{1,0},{2,1},{3,2},{4,3},{5,4},{6,5},{7,6},{8,7},{9,8},{10,9... | collective-permute-start | bytes 3538952 | tf_op jit(solution)/shard_map/ppermute | solution.py:350
  16.1 13.7 %all_to_all.15 = f32[4,3,16,1024]{3,2,1,0:T(8,128)S(1)} all-to-all(f32[4,3,16,1024]{3,2,1,0:T(8,128)S(1)} %get-tuple-element.17), channel_id=1, replica_groups={{0,16,32,48},{64,80,96,112},{1,17,33,49},{65,81,97,113},{2,18,34,50},{6..., dimensions={0} | all-to-all | bytes 1572864 | tf_op jit(solution)/shard_map/all_to_all | solution.py:352
  29.9 0.3 collective-permute-done.low
  30.2 1.8 %collective-permute-start.2 = (f32[3,16,1024]{2,1,0:T(8,128)S(1)}, f32[3,16,1024]{2,1,0:T(8,128)S(1)}, u32[]{:S(2)}, u32[]{:S(2)}) collective-permute-start(f32[3,16,1024]{2,1,0:T(8,128)S(1)} %reduce_sum.9), channel_id=1, source_target_pairs={{0,64},{16,80},{32,96},{48,112},{64,0},{80,16},{96,32},{112,48},{1... | collective-permute-start | bytes 589832 | tf_op jit(solution)/shard_map/ppermute | solution.py:357
  32.0 3.9 %collective-permute-done.2 = f32[3,16,1024]{2,1,0:T(8,128)S(1)} collective-permute-done((f32[3,16,1024]{2,1,0:T(8,128)S(1)}, f32[3,16,1024]{2,1,0:T(8,128)S(1)}, u32[]{:S(2)}, u32[]{:S(2)}) %collective-permute-start.2) | collective-permute-done | bytes 196640 | tf_op jit(solution)/shard_map/ppermute | solution.py:357
  35.9 0.1 collective-permute-start.5
  36.0 5.7 %collective-permute-start.6 = (f32[3,4,32,8,128]{4,3,2,1,0:T(8,128)}, f32[3,4,32,8,128]{4,3,2,1,0:T(8,128)S(1)}, u32[]{:S(2)}, u32[]{:S(2)}) collective-permute-start(f32[3,4,32,8,128]{4,3,2,1,0:T(8,128)} %get-tuple-element.28), channel_id=1, source_target_pairs={{0,15},{1,0},{2,1},{3,2},{4,3},{5,4},{6,5},{7,6},{8,7},{9,8},{10,9... | collective-permute-start | bytes 4718600 | tf_op jit(solution)/shard_map/ppermute | solution.py:361
  41.7 0.9 dynamic-slice_add_fusion
  42.7 0.1 broadcast_in_dim.4
  42.8 13.9 %all_to_all.16.centre = f32[4,3,16,1024]{3,2,1,0:T(8,128)S(1)} all-to-all(f32[4,3,16,1024]{3,2,1,0:T(8,128)S(1)} %broadcast_in_dim.4), channel_id=1, replica_groups={{0,16,32,48},{64,80,96,112},{1,17,33,49},{65,81,97,113},{2,18,34,50},{6..., dimensions={0} | all-to-all | bytes 1572864 | tf_op jit(solution)/shard_map/all_to_all | solution.py:363
  56.7 0.1 fusion.5
  56.8 0.1 collective-permute-start.3
  56.9 5.3 %collective-permute-start.4 = (f32[4,3,8,1024]{3,2,1,0:T(8,128)S(1)}, f32[4,3,8,1024]{3,2,1,0:T(8,128)S(1)}, u32[]{:S(2)}, u32[]{:S(2)}) collective-permute-start(f32[4,3,8,1024]{3,2,1,0:T(8,128)S(1)} %get-tuple-element.31), channel_id=1, source_target_pairs={{0,15},{1,0},{2,1},{3,2},{4,3},{5,4},{6,5},{7,6},{8,7},{9,8},{10,9... | collective-permute-start | bytes 1179656 | tf_op jit(solution)/shard_map/ppermute | solution.py:368
  62.2 5.4 %collective-permute-done.3.low_c = f32[4,3,8,1024]{3,2,1,0:T(8,128)S(1)} collective-permute-done((f32[4,3,8,1024]{3,2,1,0:T(8,128)S(1)}, f32[4,3,8,1024]{3,2,1,0:T(8,128)S(1)}, u32[]{:S(2)}, u32[]{:S(2)}) %collective-permute-start.3) | collective-permute-done | bytes 393248 | tf_op jit(solution)/shard_map/ppermute | solution.py:367
  67.7 1.2 copy-done.4
  68.9 0.4 copy-done.5
  69.3 37.7 %model.1.own = f32[4,2,8,128]{3,2,1,0:T(8,128)S(1)} custom-call(s32[4,256]{1,0:T(4,128)S(1)} %get-tuple-element.34.spots, s32[4,256]{1,0:T(4,128)S(1)} %get-tuple-element.33.turns, f32[4,3,8,1024]{3,2,1,0:T(8,128)S(1)} %collective-permute-done.3.low_c, f32[4,3,16,1024]{3,2,1,0:T(8,128)S(1)} %all_to_all.16.centre, ...), custom_call_target="tpu_custom_call" | custom-call | tf_op jit(solution)/shard_map/model/pallas_call | solution.py:270
  107.0 10.5 %all_to_all.17.every = f32[8,4,2,8,128]{4,3,2,1,0:T(8,128)} all-to-all(f32[8,4,2,8,128]{4,3,2,1,0:T(8,128)S(1)} %broadcast_in_dim.5), channel_id=1, replica_groups=mesh['mem'=8,'sp'=16] {'mem'}, dimensions={0} | all-to-all | bytes 524288 | tf_op jit(solution)/shard_map/all_to_all | solution.py:371
  117.5 2.1 %statistics.1 = (f32[8,4,256]{2,1,0:T(4,128)}, f32[64,128]{1,0:T(8,128)}) custom-call(f32[8,4,2,8,128]{4,3,2,1,0:T(8,128)} %all_to_all.17.every, f32[4,2,8,128]{3,2,1,0:T(8,128)} %copy-done, f32[4,256]{1,0:T(4,128)} %value.1, f32[4,256]{1,0:T(4,128)} %var.1), custom_call_target="tpu_custom_call" | custom-call | tf_op jit(solution)/shard_map/statistics/pallas_call | solution.py:314
  119.7 1.4 %collective-permute-done.7 = f32[64,128]{1,0:T(8,128)S(1)} collective-permute-done((f32[64,128]{1,0:T(8,128)}, f32[64,128]{1,0:T(8,128)S(1)}, u32[]{:S(2)}, u32[]{:S(2)}) %collective-permute-start.7) | collective-permute-done | bytes 32800 | tf_op jit(solution)/shard_map/ppermute | solution.py:376
  121.1 0.8 add.64
  121.9 3.9 %collective-permute-done.8 = f32[64,128]{1,0:T(8,128)S(1)} collective-permute-done((f32[64,128]{1,0:T(8,128)S(1)}, f32[64,128]{1,0:T(8,128)S(1)}, u32[]{:S(2)}, u32[]{:S(2)}) %collective-permute-start.8) | collective-permute-done | bytes 32800 | tf_op jit(solution)/shard_map/ppermute | solution.py:376
  125.8 4.0 %collective-permute-start.9 = (f32[64,128]{1,0:T(8,128)S(1)}, f32[64,128]{1,0:T(8,128)S(1)}, u32[]{:S(2)}, u32[]{:S(2)}) collective-permute-start(f32[64,128]{1,0:T(8,128)S(1)} %add.65), channel_id=1, source_target_pairs={{0,4},{1,5},{2,6},{3,7},{4,0},{5,1},{6,2},{7,3},{8,12},{9,13},{10,... | collective-permute-start | bytes 98312 | tf_op jit(solution)/shard_map/ppermute | solution.py:376
  129.8 1.9 %collective-permute-done.9 = f32[64,128]{1,0:T(8,128)S(1)} collective-permute-done((f32[64,128]{1,0:T(8,128)S(1)}, f32[64,128]{1,0:T(8,128)S(1)}, u32[]{:S(2)}, u32[]{:S(2)}) %collective-permute-start.9) | collective-permute-done | bytes 32800 | tf_op jit(solution)/shard_map/ppermute | solution.py:376
  131.7 3.2 %collective-permute-start.10 = (f32[64,128]{1,0:T(8,128)S(1)}, f32[64,128]{1,0:T(8,128)S(1)}, u32[]{:S(2)}, u32[]{:S(2)}) collective-permute-start(f32[64,128]{1,0:T(8,128)S(1)} %add.66), channel_id=1, source_target_pairs={{0,8},{1,9},{2,10},{3,11},{4,12},{5,13},{6,14},{7,15},{8,0},{9,1},... | collective-permute-start | bytes 98312 | tf_op jit(solution)/shard_map/ppermute | solution.py:376
  134.8 2.3 %collective-permute-done.10 = f32[64,128]{1,0:T(8,128)S(1)} collective-permute-done((f32[64,128]{1,0:T(8,128)S(1)}, f32[64,128]{1,0:T(8,128)S(1)}, u32[]{:S(2)}, u32[]{:S(2)}) %collective-permute-start.10) | collective-permute-done | bytes 32800 | tf_op jit(solution)/shard_map/ppermute | solution.py:376
  137.1 0.6 slice_add_fusion
  137.7 0.2 slice_reduce_fusion
  137.9 0.5 multiply_subtract_fusion
  (34 shorter events, 0.2 us)
Async XLA Ops:
  0.6 0.7 copy-start.2
  10.5 19.7 %collective-permute-start = (f32[3,3,32,8,128]{4,3,2,1,0:T(8,128)}, f32[3,3,32,8,128]{4,3,2,1,0:T(8,128)S(1)}, u32[]{:S(2)}, u32[]{:S(2)}) collective-permute-start(f32[3,3,32,8,128]{4,3,2,1,0:T(8,128)} %get-tuple-element.18), channel_id=1, source_target_pairs={{0,1},{1,2},{2,3},{3,4},{4,5},{5,6},{6,7},{7,8},{8,9},{9,10},{10,1... | collective-permute-start | bytes 3538952 | tf_op jit(solution)/shard_map/ppermute | solution.py:349
  10.5 19.7 %collective-permute-start.1 = (f32[3,3,32,8,128]{4,3,2,1,0:T(8,128)}, f32[3,3,32,8,128]{4,3,2,1,0:T(8,128)S(1)}, u32[]{:S(2)}, u32[]{:S(2)}) collective-permute-start(f32[3,3,32,8,128]{4,3,2,1,0:T(8,128)} %get-tuple-element.19), channel_id=1, source_target_pairs={{0,15},{1,0},{2,1},{3,2},{4,3},{5,4},{6,5},{7,6},{8,7},{9,8},{10,9... | collective-permute-start | bytes 3538952 | tf_op jit(solution)/shard_map/ppermute | solution.py:350
  30.1 5.8 %copy-start.6 = (f32[3,3,32,8,128]{4,3,2,1,0:T(8,128)}, f32[3,3,32,8,128]{4,3,2,1,0:T(8,128)S(1)}, u32[]{:S(2)}) copy-start(f32[3,3,32,8,128]{4,3,2,1,0:T(8,128)S(1)} %collective-permute-done.low) | copy-start | bytes 3538948
  30.1 5.8 %copy-start.7 = (f32[3,3,32,8,128]{4,3,2,1,0:T(8,128)}, f32[3,3,32,8,128]{4,3,2,1,0:T(8,128)S(1)}, u32[]{:S(2)}) copy-start(f32[3,3,32,8,128]{4,3,2,1,0:T(8,128)S(1)} %collective-permute-done.1.high) | copy-start | bytes 3538948
  30.2 5.7 %collective-permute-start.2 = (f32[3,16,1024]{2,1,0:T(8,128)S(1)}, f32[3,16,1024]{2,1,0:T(8,128)S(1)}, u32[]{:S(2)}, u32[]{:S(2)}) collective-permute-start(f32[3,16,1024]{2,1,0:T(8,128)S(1)} %reduce_sum.9), channel_id=1, source_target_pairs={{0,64},{16,80},{32,96},{48,112},{64,0},{80,16},{96,32},{112,48},{1... | collective-permute-start | bytes 589832 | tf_op jit(solution)/shard_map/ppermute | solution.py:357
  35.9 31.7 %collective-permute-start.5 = (f32[3,4,32,8,128]{4,3,2,1,0:T(8,128)}, f32[3,4,32,8,128]{4,3,2,1,0:T(8,128)S(1)}, u32[]{:S(2)}, u32[]{:S(2)}) collective-permute-start(f32[3,4,32,8,128]{4,3,2,1,0:T(8,128)} %get-tuple-element.26), channel_id=1, source_target_pairs={{0,1},{1,2},{2,3},{3,4},{4,5},{5,6},{6,7},{7,8},{8,9},{9,10},{10,1... | collective-permute-start | bytes 4718600 | tf_op jit(solution)/shard_map/ppermute | solution.py:360
  36.0 31.6 %collective-permute-start.6 = (f32[3,4,32,8,128]{4,3,2,1,0:T(8,128)}, f32[3,4,32,8,128]{4,3,2,1,0:T(8,128)S(1)}, u32[]{:S(2)}, u32[]{:S(2)}) collective-permute-start(f32[3,4,32,8,128]{4,3,2,1,0:T(8,128)} %get-tuple-element.28), channel_id=1, source_target_pairs={{0,15},{1,0},{2,1},{3,2},{4,3},{5,4},{6,5},{7,6},{8,7},{9,8},{10,9... | collective-permute-start | bytes 4718600 | tf_op jit(solution)/shard_map/ppermute | solution.py:361
  42.8 19.4 %copy-start.8 = (s32[4,256]{1,0:T(4,128)S(1)}, s32[4,256]{1,0:T(4,128)}, u32[]{:S(2)}) copy-start(s32[4,256]{1,0:T(4,128)} %param.16) | copy-start | bytes 12292
  42.8 19.4 %copy-start.9 = (s32[4,256]{1,0:T(4,128)S(1)}, s32[4,256]{1,0:T(4,128)}, u32[]{:S(2)}) copy-start(s32[4,256]{1,0:T(4,128)} %param.15) | copy-start | bytes 12292
  42.8 19.4 %copy-start.10 = (s32[256]{0:T(256)S(1)}, s32[256]{0:T(256)}, u32[]{:S(2)}) copy-start(s32[256]{0:T(256)} %param.14) | copy-start | bytes 3076
  42.8 19.4 %copy-start.11 = (s32[256]{0:T(256)S(1)}, s32[256]{0:T(256)}, u32[]{:S(2)}) copy-start(s32[256]{0:T(256)} %param.13) | copy-start | bytes 3076
  42.8 26.5 %copy-start.1 = (f32[4,256]{1,0:T(4,128)S(1)}, f32[4,256]{1,0:T(4,128)}, u32[]{:S(2)}) copy-start(f32[4,256]{1,0:T(4,128)} %obs_weight.1) | copy-start | bytes 12292
  56.8 10.9 %collective-permute-start.3 = (f32[4,3,8,1024]{3,2,1,0:T(8,128)S(1)}, f32[4,3,8,1024]{3,2,1,0:T(8,128)S(1)}, u32[]{:S(2)}, u32[]{:S(2)}) collective-permute-start(f32[4,3,8,1024]{3,2,1,0:T(8,128)S(1)} %get-tuple-element.32), channel_id=1, source_target_pairs={{0,1},{1,2},{2,3},{3,4},{4,5},{5,6},{6,7},{7,8},{8,9},{9,10},{10,1... | collective-permute-start | bytes 1179656 | tf_op jit(solution)/shard_map/ppermute | solution.py:367
  56.9 10.8 %collective-permute-start.4 = (f32[4,3,8,1024]{3,2,1,0:T(8,128)S(1)}, f32[4,3,8,1024]{3,2,1,0:T(8,128)S(1)}, u32[]{:S(2)}, u32[]{:S(2)}) collective-permute-start(f32[4,3,8,1024]{3,2,1,0:T(8,128)S(1)} %get-tuple-element.31), channel_id=1, source_target_pairs={{0,15},{1,0},{2,1},{3,2},{4,3},{5,4},{6,5},{7,6},{8,7},{9,8},{10,9... | collective-permute-start | bytes 1179656 | tf_op jit(solution)/shard_map/ppermute | solution.py:368
  67.7 1.3 copy-start.4
  67.7 1.7 %copy-start.5 = (f32[3,4,32,8,128]{4,3,2,1,0:T(8,128)}, f32[3,4,32,8,128]{4,3,2,1,0:T(8,128)S(1)}, u32[]{:S(2)}) copy-start(f32[3,4,32,8,128]{4,3,2,1,0:T(8,128)S(1)} %collective-permute-done.6.high_more) | copy-start | bytes 4718596
  107.0 10.5 %copy-start = (f32[4,2,8,128]{3,2,1,0:T(8,128)}, f32[4,2,8,128]{3,2,1,0:T(8,128)S(1)}, u32[]{:S(2)}) copy-start(f32[4,2,8,128]{3,2,1,0:T(8,128)S(1)} %model.1.own) | copy-start | bytes 98308
  107.0 30.9 %copy-start.3 = (f32[64]{0:T(128)S(1)}, f32[64]{0:T(128)}, u32[]{:S(2)}) copy-start(f32[64]{0:T(128)} %weights.1) | copy-start | bytes 772
  119.7 1.4 %collective-permute-start.7 = (f32[64,128]{1,0:T(8,128)}, f32[64,128]{1,0:T(8,128)S(1)}, u32[]{:S(2)}, u32[]{:S(2)}) collective-permute-start(f32[64,128]{1,0:T(8,128)} %get-tuple-element.30), channel_id=1, source_target_pairs={{0,1},{1,0},{2,3},{3,2},{4,5},{5,4},{6,7},{7,6},{8,9},{9,8},{10,11... | collective-permute-start | bytes 98312 | tf_op jit(solution)/shard_map/ppermute | solution.py:376
  121.8 3.9 %collective-permute-start.8 = (f32[64,128]{1,0:T(8,128)S(1)}, f32[64,128]{1,0:T(8,128)S(1)}, u32[]{:S(2)}, u32[]{:S(2)}) collective-permute-start(f32[64,128]{1,0:T(8,128)S(1)} %add.64), channel_id=1, source_target_pairs={{0,2},{1,3},{2,0},{3,1},{4,6},{5,7},{6,4},{7,5},{8,10},{9,11},{10,... | collective-permute-start | bytes 98312 | tf_op jit(solution)/shard_map/ppermute | solution.py:376
  125.8 5.9 %collective-permute-start.9 = (f32[64,128]{1,0:T(8,128)S(1)}, f32[64,128]{1,0:T(8,128)S(1)}, u32[]{:S(2)}, u32[]{:S(2)}) collective-permute-start(f32[64,128]{1,0:T(8,128)S(1)} %add.65), channel_id=1, source_target_pairs={{0,4},{1,5},{2,6},{3,7},{4,0},{5,1},{6,2},{7,3},{8,12},{9,13},{10,... | collective-permute-start | bytes 98312 | tf_op jit(solution)/shard_map/ppermute | solution.py:376
  131.7 5.4 %collective-permute-start.10 = (f32[64,128]{1,0:T(8,128)S(1)}, f32[64,128]{1,0:T(8,128)S(1)}, u32[]{:S(2)}, u32[]{:S(2)}) collective-permute-start(f32[64,128]{1,0:T(8,128)S(1)} %add.66), channel_id=1, source_target_pairs={{0,8},{1,9},{2,10},{3,11},{4,12},{5,13},{6,14},{7,15},{8,0},{9,1},... | collective-permute-start | bytes 98312 | tf_op jit(solution)/shard_map/ppermute | solution.py:376

commit v3 on v2

--- a/solution.py
+++ b/solution.py
@@ -1,3 +1,5 @@
+import functools
+
 import jax
 import jax.numpy as jnp
 from jax import lax
@@ -10,7 +12,7 @@
 EARLY = 3
 LANES = 128
 GROUP = 4
-PAIR = 2
+PAIR = 4
 SPAN = 4
 NEAR = 4
 VMEM_MODEL = 38 << 20
@@ -30,40 +32,39 @@
     return [(i, (i + step) % count) for i in range(count)]
 
 
-def prepare_kernel(place, weights, anom, turned, top, top_more, bottom, bottom_more, partial):
-    members, rows = anom.shape[0], anom.shape[2]
+def prepare_kernel(place, weights, anom, *outs):
+    *parts, partial = outs
+    members, half = anom.shape[0], anom.shape[2]
     chunks, width = partial.shape[0], partial.shape[3]
     first = place[0] * members
     scales = [weights[first + m] for m in range(members)]
-
     per = width // (SPAN * LANES)
-
-    def columns(c, carry):
-        swapped, totals = [], []
-        for i in range(SPAN):
-            block = anom[:, 0, :, pl.ds(pl.multiple_of((c * SPAN + i) * LANES, LANES), LANES)]
-            swapped.append(jnp.swapaxes(block, 0, 1))
-            total = scales[0] * block[0]
-            for m in range(1, members):
-                total = total + scales[m] * block[m]
-            totals.append(total)
-        inner = pl.multiple_of(lax.rem(c, per) * (SPAN * LANES), SPAN * LANES)
-        for i in range(SPAN):
-            turned[0, :, c * SPAN + i] = swapped[i]
-            partial[lax.div(c, per), 0, :, pl.ds(inner + i * LANES, LANES)] = totals[i]
-        return carry
-
-    lax.fori_loop(0, chunks * per, columns, 0)
-
-    @pl.when(pl.program_id(1) == 0)
-    def _():
-        top[0] = turned[0, :EARLY]
-        top_more[0] = turned[0, EARLY:HALO]
-
-    @pl.when(pl.program_id(1) == 1)
-    def _():
-        bottom[0] = turned[0, rows - HALO : rows - HALO + EARLY]
-        bottom_more[0] = turned[0, rows - HALO + EARLY :]
+    homes = [(part, r) for part in parts for r in range(part.shape[1])]
+
+    def turn(homes):
+        def columns(c, carry):
+            swapped, totals = [], []
+            for i in range(SPAN):
+                block = anom[:, 0, :, pl.ds(pl.multiple_of((c * SPAN + i) * LANES, LANES), LANES)]
+                swapped.append(jnp.swapaxes(block, 0, 1))
+                total = scales[0] * block[0]
+                for m in range(1, members):
+                    total = total + scales[m] * block[m]
+                totals.append(total)
+            inner = pl.multiple_of(lax.rem(c, per) * (SPAN * LANES), SPAN * LANES)
+            for i in range(SPAN):
+                for r, (part, home) in enumerate(homes):
+                    part[0, home, c * SPAN + i] = swapped[i][r]
+                partial[lax.div(c, per), 0, :, pl.ds(inner + i * LANES, LANES)] = totals[i]
+            return carry
+
+        lax.fori_loop(0, chunks * per, columns, 0)
+
+    for step in range(2):
+
+        @pl.when(pl.program_id(1) == step)
+        def _():
+            turn(homes[step * half : (step + 1) * half])
 
 
 def prepare(place, weights, anomalies):
@@ -73,18 +74,17 @@
     width = columns // chunks
     smem = pl.BlockSpec(memory_space=pltpu.SMEM)
     tiles = columns // LANES
-    parts = (EARLY, HALO - EARLY) * 2
+    late = HALO - EARLY
+    parts = (EARLY, late, rows - 2 * HALO, EARLY, late)
     return pl.pallas_call(
         prepare_kernel,
         grid=(fields, 2),
         in_specs=[smem, smem, pl.BlockSpec((members, 1, half, columns), lambda f, r: (0, f, r, 0))],
         out_specs=[
-            pl.BlockSpec((1, half, tiles, members, LANES), lambda f, r: (f, r, 0, 0, 0)),
             *(pl.BlockSpec((1, part, tiles, members, LANES), lambda f, r: (f, 0, 0, 0, 0)) for part in parts),
             pl.BlockSpec((chunks, 1, half, width), lambda f, r: (0, f, r, 0)),
         ],
         out_shape=[
-            pltpu.HBM((fields, rows, tiles, members, LANES), jnp.float32),
             *(pltpu.HBM((fields, part, tiles, members, LANES), jnp.float32) for part in parts),
             jax.ShapeDtypeStruct((chunks, fields, rows, width), jnp.float32),
         ],
@@ -94,22 +94,20 @@
 
 
 def model_kernel(
-    spots, turns, low_c, centre, high_c, obs_weight, own, low, low_more, high, high_more, out, state, heights, spare, sems
+    spots, turns, low_c, centre, high_c, obs_weight, *refs
 ):
-    rows, tiles = own.shape[1], own.shape[2]
-    tall = rows + 2 * HALO
+    *sources, out, state, heights, spare, sems = refs
+    tall, tiles = state.shape[1], state.shape[2]
+    rows = tall - 2 * HALO
     copies = []
-    row = 0
-    for source in (low, low_more, own, high, high_more):
-        part = source.shape[1]
-        for f in range(3):
-            target = state.at[f, pl.ds(row, part)]
-            copies.append(pltpu.make_async_copy(source.at[f], target, sems.at[len(copies)]))
-        row += part
+    for f in range(3):
+        row = 0
+        for i, source in enumerate(sources):
+            part = source.shape[1]
+            copies.append(pltpu.make_async_copy(source.at[f], state.at[f, pl.ds(row, part)], sems.at[f, i]))
+            row += part
     for copy in copies:
         copy.start()
-    for copy in copies:
-        copy.wait()
 
     lane = lax.broadcasted_iota(jnp.int32, (8, LANES), 1)
     is_first = lane == 0
@@ -119,9 +117,8 @@
 
     edge = low_c.shape[2]
 
-    def begin(i, carry):
-        f = lax.div(i, tiles // PAIR)
-        first = lax.rem(i, tiles // PAIR) * PAIR
+    def begin(f, i, carry):
+        first = i * PAIR
         chunk = lax.div(first, per)
         inner = pl.multiple_of(lax.rem(first, per) * LANES, PAIR * LANES)
         for base, skip, at, count in (
@@ -138,7 +135,10 @@
                 state[f, at + r, first + t] = value
         return carry
 
-    lax.fori_loop(0, 3 * tiles // PAIR, begin, 0)
+    for f in range(3):
+        for copy in copies[f * len(sources) : (f + 1) * len(sources)]:
+            copy.wait()
+        lax.fori_loop(0, tiles // PAIR, functools.partial(begin, f), 0)
 
     def memo(fetch):
         kept = {}
@@ -185,7 +185,7 @@
 
             return value
 
-        sweep([row(i) for i in range(ROWS)], (hn,), r)
+        sweep([row(i) for i in range(2 * ROWS)], (hn,), r)
 
     def momentum_rows(h, u, v, un, vn, r):
         gh, gu, gv = rows_of(h, r), rows_of(u, r), rows_of(v, r)
@@ -223,10 +223,10 @@
         fresh = (heights, step)
 
         def height_body(i, carry):
-            height_rows(reader(*h), reader(*u), reader(*v), writer(*fresh), low_row + ROWS * i)
+            height_rows(reader(*h), reader(*u), reader(*v), writer(*fresh), low_row + 2 * ROWS * i)
             return carry
 
-        lax.fori_loop(0, (tall - 2 * low_row) // ROWS, height_body, 0)
+        lax.fori_loop(0, (tall - 2 * low_row) // (2 * ROWS), height_body, 0)
         if step + 1 < STEPS:
 
             def momentum_body(i, carry):
@@ -261,26 +261,26 @@
             out[step, group] = total
 
 
-def run_model(spots, turns, low_c, centre, high_c, obs_weight, own, *halos):
-    fields, rows, tiles, members, _ = own.shape
-    tall = rows + 2 * HALO
+def run_model(spots, turns, low_c, centre, high_c, obs_weight, *parts):
+    fields, _, tiles, members, _ = parts[0].shape
+    tall = sum(part.shape[1] for part in parts)
     smem = pl.BlockSpec(memory_space=pltpu.SMEM)
     vmem = pl.BlockSpec(memory_space=pltpu.VMEM)
     groups = obs_weight.shape[1] // LANES
     return pl.pallas_call(
         model_kernel,
-        in_specs=[smem, smem] + [vmem] * 4 + [pl.BlockSpec(memory_space=pltpu.HBM)] * 5,
+        in_specs=[smem, smem] + [vmem] * 4 + [pl.BlockSpec(memory_space=pl.ANY)] * len(parts),
         out_specs=vmem,
         out_shape=jax.ShapeDtypeStruct((STEPS, groups, members, LANES), jnp.float32),
         scratch_shapes=[
             pltpu.VMEM((fields, tall, tiles, members, LANES), jnp.float32),
             pltpu.VMEM((STEPS, tall, tiles, members, LANES), jnp.float32),
             pltpu.VMEM((2, tall, tiles, members, LANES), jnp.float32),
-            pltpu.SemaphoreType.DMA((15,)),
+            pltpu.SemaphoreType.DMA((fields, len(parts))),
         ],
         compiler_params=pltpu.CompilerParams(vmem_limit_bytes=VMEM_MODEL),
         name="model",
-    )(spots, turns, low_c, centre, high_c, obs_weight, own, *halos)
+    )(spots, turns, low_c, centre, high_c, obs_weight, *parts)
 
 
 def statistics_kernel(every, own, value, var, anom, packed):
@@ -345,7 +345,8 @@
     slot = jnp.arange(col.shape[1], dtype=jnp.int32)[None, :]
     turns = (slot - col) % LANES
 
-    own, top, top_more, bottom, bottom_more, partial_sum = prepare(place.reshape(1), weights, in_hbm(anomalies))
+    top, top_more, middle, bottom, bottom_more, partial_sum = prepare(place.reshape(1), weights, in_hbm(anomalies))
+    own = [in_hbm(part) for part in (top, top_more, middle, bottom, bottom_more)]
     low = lax.ppermute(bottom, "sp", ring("sp", 1))
     high = lax.ppermute(top, "sp", ring("sp", -1))
 
@@ -367,7 +368,7 @@
     low_c = lax.ppermute(centre[:, :, rows - edge :], "sp", ring("sp", 1))
     high_c = lax.ppermute(centre[:, :, :edge], "sp", ring("sp", -1))
 
-    seen = run_model(spots, turns, low_c, centre, high_c, obs_weight, *map(in_hbm, (own, low, low_more, high, high_more)))
+    seen = run_model(spots, turns, low_c, centre, high_c, obs_weight, in_hbm(low), low_more, *own, in_hbm(high), high_more)
     every = lax.all_to_all(jnp.broadcast_to(seen[None], (count, *seen.shape)), "mem", 0, 0, tiled=True)
     obs_anom, packed = statistics(every, seen, obs_value, obs_var)
     count = lax.axis_size("sp")

time: 140 us -> 135 us (0.964)
  waiting for transfers between devices: 19.1 us -> 27.7 us
  starting transfers between devices: 25.8 us -> 18.7 us
  Pallas kernels: 49 us -> 44 us
  local copies, waits for them, and re-layouts: 2.67 us -> 1.02 us
    ppermute x1, waiting for transfers between devices: 0.01 us -> 5.24 us  [body(): high_c = lax.ppermute(centre[:, :, :edge], 'sp', ring('sp', -1))]
    pallas_call x1, Pallas kernels: 37.7 us -> 33.8 us  [run_model(): pl.pallas_call(model_kernel, in_specs=[smem, smem] + [vmem] * 4 + [pl.Blo...]
    ppermute x4, starting transfers between devices: 7.14 us -> 3.44 us  [body(): lax.ppermute(packed, 'sp', [(i, i ^ hop) for i in range(count)])]
    ppermute x1, starting transfers between devices: 5.35 us -> 2.06 us  [body(): high_c = lax.ppermute(centre[:, :, :edge], 'sp', ring('sp', -1))]
    ppermute x4, waiting for transfers between devices: 9.49 us -> 12.7 us  [body(): lax.ppermute(packed, 'sp', [(i, i ^ hop) for i in range(count)])]
    unnamed x24 -> x20, local copies, waits for them, and re-layouts: 2.35 us -> 0.7 us
  transfers between devices with their start and end apart: 11 -> 11, of which waited for: 7 -> 8; matrix products, arithmetic and copies ran while one was open for 1% -> 1% of each run, Pallas kernels for 0% -> 0%
where the time goes in v3:
time: 135 us; the launch traced here: 134 us
  Pallas kernels  44 us (33%)
  blocking collectives  39.1 us (29%)
  waiting for transfers between devices  27.7 us (21%)
  starting transfers between devices  18.7 us (14%)
  other arithmetic  2.97 us (2%)
    pallas_call x1, Pallas kernels, run_model(): pl.pallas_call(model_kernel, in_specs=[smem, smem] + [vmem] * 4 + [pl.Blo...  33.8 us
    all_to_all x1, blocking collectives, body(): lax.all_to_all(jnp.broadcast_to(piece[None], (NEAR, *piece.shape)), 'mem'...  13.9 us
    all_to_all x1, blocking collectives, body(): lax.all_to_all(partial_sum, 'mem', 0, 0, axis_index_groups=near, tiled=True)  13.7 us
    ppermute x4, waiting for transfers between devices, body(): lax.ppermute(packed, 'sp', [(i, i ^ hop) for i in range(count)])  12.7 us
    all_to_all x1, blocking collectives, body(): lax.all_to_all(jnp.broadcast_to(seen[None], (count, *seen.shape)), 'mem',...  11.4 us
    pallas_call x1, Pallas kernels, prepare(): pl.pallas_call(prepare_kernel, grid=(fields, 2), in_specs=[smem, smem, pl...  8.11 us
    ppermute x1, starting transfers between devices, body(): high_more = lax.ppermute(top_more, 'sp', ring('sp', -1))  5.71 us
    ppermute x1, starting transfers between devices, body(): high = lax.ppermute(top, 'sp', ring('sp', -1))  5.61 us
  transfers between devices with their start and end apart: 11, of which 8 were waited for; matrix products, arithmetic and copies ran while one was open for 1% of the time, Pallas kernels for 0%

profile of v3, /device:TPU:0, one launch (start us, length us, event | category | flops | bytes accessed | tf_op | source)
XLA Modules:
  0.0 134.3 jit_solution(718496858720198757)
XLA Ops:
  0.6 0.0 copy-start.2
  0.6 0.6 copy-done.2
  1.3 8.1 %prepare.1 = (f32[3,3,32,8,128]{4,3,2,1,0:T(8,128)}, f32[3,4,32,8,128]{4,3,2,1,0:T(8,128)}, f32[3,2,32,8,128]{4,3,2,1,0:T(8,128)}, f32[3,3,32,8,128]{4,3,2,1,0:T...) custom-call(s32[1]{0:T(128)} %bitcast.place, f32[64]{0:T(128)S(1)} %copy-done.2, ...), custom_call_target="tpu_custom_call" | custom-call | tf_op jit(solution)/shard_map/prepare/pallas_call | solution.py:79
  9.4 5.6 %collective-permute-start.1 = (f32[3,3,32,8,128]{4,3,2,1,0:T(8,128)}, f32[3,3,32,8,128]{4,3,2,1,0:T(8,128)S(1)}, u32[]{:S(2)}, u32[]{:S(2)}) collective-permute-start(f32[3,3,32,8,128]{4,3,2,1,0:T(8,128)} %get-tuple-element.19.refs_2_), channel_id=1, source_target_pairs={{0,15},{1,0},{2,1},{3,2},{4,3},{5,4},{6,5},{7,6},{8,7},{9,8},{10,9... | collective-permute-start | bytes 3538952 | tf_op jit(solution)/shard_map/ppermute | solution.py:351
  15.0 13.7 %all_to_all.15 = f32[4,3,16,1024]{3,2,1,0:T(8,128)S(1)} all-to-all(f32[4,3,16,1024]{3,2,1,0:T(8,128)S(1)} %get-tuple-element.17), channel_id=1, replica_groups={{0,16,32,48},{64,80,96,112},{1,17,33,49},{65,81,97,113},{2,18,34,50},{6..., dimensions={0} | all-to-all | bytes 1572864 | tf_op jit(solution)/shard_map/all_to_all | solution.py:353
  28.8 0.3 collective-permute-done.refs_0_
  29.1 1.8 %collective-permute-start.2 = (f32[3,16,1024]{2,1,0:T(8,128)S(1)}, f32[3,16,1024]{2,1,0:T(8,128)S(1)}, u32[]{:S(2)}, u32[]{:S(2)}) collective-permute-start(f32[3,16,1024]{2,1,0:T(8,128)S(1)} %reduce_sum.9), channel_id=1, source_target_pairs={{0,64},{16,80},{32,96},{48,112},{64,0},{80,16},{96,32},{112,48},{1... | collective-permute-start | bytes 589832 | tf_op jit(solution)/shard_map/ppermute | solution.py:358
  30.9 3.9 %collective-permute-done.2 = f32[3,16,1024]{2,1,0:T(8,128)S(1)} collective-permute-done((f32[3,16,1024]{2,1,0:T(8,128)S(1)}, f32[3,16,1024]{2,1,0:T(8,128)S(1)}, u32[]{:S(2)}, u32[]{:S(2)}) %collective-permute-start.2) | collective-permute-done | bytes 196640 | tf_op jit(solution)/shard_map/ppermute | solution.py:358
  34.9 0.1 collective-permute-start.5
  35.0 5.7 %collective-permute-start.6 = (f32[3,4,32,8,128]{4,3,2,1,0:T(8,128)}, f32[3,4,32,8,128]{4,3,2,1,0:T(8,128)S(1)}, u32[]{:S(2)}, u32[]{:S(2)}) collective-permute-start(f32[3,4,32,8,128]{4,3,2,1,0:T(8,128)} %get-tuple-element.28.refs_3_), channel_id=1, source_target_pairs={{0,15},{1,0},{2,1},{3,2},{4,3},{5,4},{6,5},{7,6},{8,7},{9,8},{10,9... | collective-permute-start | bytes 4718600 | tf_op jit(solution)/shard_map/ppermute | solution.py:362
  40.7 0.9 dynamic-slice_add_fusion
  41.6 0.1 broadcast_in_dim.4
  41.7 0.0 copy-start.6
  41.7 0.0 copy-start.7
  41.8 0.0 copy-start.1
  41.8 13.9 %all_to_all.16.centre = f32[4,3,16,1024]{3,2,1,0:T(8,128)S(1)} all-to-all(f32[4,3,16,1024]{3,2,1,0:T(8,128)S(1)} %broadcast_in_dim.4), channel_id=1, replica_groups={{0,16,32,48},{64,80,96,112},{1,17,33,49},{65,81,97,113},{2,18,34,50},{6..., dimensions={0} | all-to-all | bytes 1572864 | tf_op jit(solution)/shard_map/all_to_all | solution.py:364
  55.7 0.1 fusion.5
  55.7 2.1 %collective-permute-start.4 = (f32[4,3,8,1024]{3,2,1,0:T(8,128)S(1)}, f32[4,3,8,1024]{3,2,1,0:T(8,128)S(1)}, u32[]{:S(2)}, u32[]{:S(2)}) collective-permute-start(f32[4,3,8,1024]{3,2,1,0:T(8,128)S(1)} %get-tuple-element.31), channel_id=1, source_target_pairs={{0,15},{1,0},{2,1},{3,2},{4,3},{5,4},{6,5},{7,6},{8,7},{9,8},{10,9... | collective-permute-start | bytes 1179656 | tf_op jit(solution)/shard_map/ppermute | solution.py:369
  57.8 5.2 %collective-permute-done.4.high_c = f32[4,3,8,1024]{3,2,1,0:T(8,128)S(1)} collective-permute-done((f32[4,3,8,1024]{3,2,1,0:T(8,128)S(1)}, f32[4,3,8,1024]{3,2,1,0:T(8,128)S(1)}, u32[]{:S(2)}, u32[]{:S(2)}) %collective-permute-start.4) | collective-permute-done | bytes 393248 | tf_op jit(solution)/shard_map/ppermute | solution.py:369
  63.1 5.5 %collective-permute-done.3.low_c = f32[4,3,8,1024]{3,2,1,0:T(8,128)S(1)} collective-permute-done((f32[4,3,8,1024]{3,2,1,0:T(8,128)S(1)}, f32[4,3,8,1024]{3,2,1,0:T(8,128)S(1)}, u32[]{:S(2)}, u32[]{:S(2)}) %collective-permute-start.3) | collective-permute-done | bytes 393248 | tf_op jit(solution)/shard_map/ppermute | solution.py:368
  68.6 33.8 %model.1.own = f32[4,2,8,128]{3,2,1,0:T(8,128)S(1)} custom-call(s32[4,256]{1,0:T(4,128)S(1)} %get-tuple-element.34.spots, s32[4,256]{1,0:T(4,128)S(1)} %get-tuple-element.33.turns, f32[4,3,8,1024]{3,2,1,0:T(8,128)S(1)} %collective-permute-done.3.low_c, f32[4,3,16,1024]{3,2,1,0:T(8,128)S(1)} %all_to_all.16.centre, ...), custom_call_target="tpu_custom_call" | custom-call | tf_op jit(solution)/shard_map/model/pallas_call | solution.py:270
  102.5 11.4 %all_to_all.17.every = f32[8,4,2,8,128]{4,3,2,1,0:T(8,128)} all-to-all(f32[8,4,2,8,128]{4,3,2,1,0:T(8,128)S(1)} %broadcast_in_dim.5), channel_id=1, replica_groups=mesh['mem'=8,'sp'=16] {'mem'}, dimensions={0} | all-to-all | bytes 524288 | tf_op jit(solution)/shard_map/all_to_all | solution.py:372
  113.9 2.1 %statistics.1 = (f32[8,4,256]{2,1,0:T(4,128)}, f32[64,128]{1,0:T(8,128)}) custom-call(f32[8,4,2,8,128]{4,3,2,1,0:T(8,128)} %all_to_all.17.every, f32[4,2,8,128]{3,2,1,0:T(8,128)} %copy-done, f32[4,256]{1,0:T(4,128)} %value.1, f32[4,256]{1,0:T(4,128)} %var.1), custom_call_target="tpu_custom_call" | custom-call | tf_op jit(solution)/shard_map/statistics/pallas_call | solution.py:314
  116.0 1.4 %collective-permute-done.7 = f32[64,128]{1,0:T(8,128)S(1)} collective-permute-done((f32[64,128]{1,0:T(8,128)}, f32[64,128]{1,0:T(8,128)S(1)}, u32[]{:S(2)}, u32[]{:S(2)}) %collective-permute-start.7) | collective-permute-done | bytes 32800 | tf_op jit(solution)/shard_map/ppermute | solution.py:377
  117.4 0.8 add.64
  118.2 3.9 %collective-permute-done.8 = f32[64,128]{1,0:T(8,128)S(1)} collective-permute-done((f32[64,128]{1,0:T(8,128)S(1)}, f32[64,128]{1,0:T(8,128)S(1)}, u32[]{:S(2)}, u32[]{:S(2)}) %collective-permute-start.8) | collective-permute-done | bytes 32800 | tf_op jit(solution)/shard_map/ppermute | solution.py:377
  122.1 5.4 %collective-permute-done.9 = f32[64,128]{1,0:T(8,128)S(1)} collective-permute-done((f32[64,128]{1,0:T(8,128)S(1)}, f32[64,128]{1,0:T(8,128)S(1)}, u32[]{:S(2)}, u32[]{:S(2)}) %collective-permute-start.9) | collective-permute-done | bytes 32800 | tf_op jit(solution)/shard_map/ppermute | solution.py:377
  127.6 3.4 %collective-permute-start.10 = (f32[64,128]{1,0:T(8,128)S(1)}, f32[64,128]{1,0:T(8,128)S(1)}, u32[]{:S(2)}, u32[]{:S(2)}) collective-permute-start(f32[64,128]{1,0:T(8,128)S(1)} %add.66), channel_id=1, source_target_pairs={{0,8},{1,9},{2,10},{3,11},{4,12},{5,13},{6,14},{7,15},{8,0},{9,1},... | collective-permute-start | bytes 98312 | tf_op jit(solution)/shard_map/ppermute | solution.py:377
  131.0 2.0 %collective-permute-done.10 = f32[64,128]{1,0:T(8,128)S(1)} collective-permute-done((f32[64,128]{1,0:T(8,128)S(1)}, f32[64,128]{1,0:T(8,128)S(1)}, u32[]{:S(2)}, u32[]{:S(2)}) %collective-permute-start.10) | collective-permute-done | bytes 32800 | tf_op jit(solution)/shard_map/ppermute | solution.py:377
  133.0 0.2 slice_reduce_fusion
  133.2 0.6 slice_add_fusion
  133.8 0.5 multiply_subtract_fusion
  (30 shorter events, 0.2 us)
Async XLA Ops:
  0.6 0.7 copy-start.2
  9.4 19.7 %collective-permute-start = (f32[3,3,32,8,128]{4,3,2,1,0:T(8,128)}, f32[3,3,32,8,128]{4,3,2,1,0:T(8,128)S(1)}, u32[]{:S(2)}, u32[]{:S(2)}) collective-permute-start(f32[3,3,32,8,128]{4,3,2,1,0:T(8,128)} %get-tuple-element.18.refs_5_), channel_id=1, source_target_pairs={{0,1},{1,2},{2,3},{3,4},{4,5},{5,6},{6,7},{7,8},{8,9},{9,10},{10,1... | collective-permute-start | bytes 3538952 | tf_op jit(solution)/shard_map/ppermute | solution.py:350
  9.4 19.7 %collective-permute-start.1 = (f32[3,3,32,8,128]{4,3,2,1,0:T(8,128)}, f32[3,3,32,8,128]{4,3,2,1,0:T(8,128)S(1)}, u32[]{:S(2)}, u32[]{:S(2)}) collective-permute-start(f32[3,3,32,8,128]{4,3,2,1,0:T(8,128)} %get-tuple-element.19.refs_2_), channel_id=1, source_target_pairs={{0,15},{1,0},{2,1},{3,2},{4,3},{5,4},{6,5},{7,6},{8,7},{9,8},{10,9... | collective-permute-start | bytes 3538952 | tf_op jit(solution)/shard_map/ppermute | solution.py:351
  29.1 5.8 %copy-start.4 = (f32[3,3,32,8,128]{4,3,2,1,0:T(8,128)}, f32[3,3,32,8,128]{4,3,2,1,0:T(8,128)S(1)}, u32[]{:S(2)}) copy-start(f32[3,3,32,8,128]{4,3,2,1,0:T(8,128)S(1)} %collective-permute-done.refs_0_) | copy-start | bytes 3538948
  29.1 5.8 %copy-start.5 = (f32[3,3,32,8,128]{4,3,2,1,0:T(8,128)}, f32[3,3,32,8,128]{4,3,2,1,0:T(8,128)S(1)}, u32[]{:S(2)}) copy-start(f32[3,3,32,8,128]{4,3,2,1,0:T(8,128)S(1)} %collective-permute-done.1.refs_7_) | copy-start | bytes 3538948
  29.1 5.7 %collective-permute-start.2 = (f32[3,16,1024]{2,1,0:T(8,128)S(1)}, f32[3,16,1024]{2,1,0:T(8,128)S(1)}, u32[]{:S(2)}, u32[]{:S(2)}) collective-permute-start(f32[3,16,1024]{2,1,0:T(8,128)S(1)} %reduce_sum.9), channel_id=1, source_target_pairs={{0,64},{16,80},{32,96},{48,112},{64,0},{80,16},{96,32},{112,48},{1... | collective-permute-start | bytes 589832 | tf_op jit(solution)/shard_map/ppermute | solution.py:358
  34.9 33.7 %collective-permute-start.5 = (f32[3,4,32,8,128]{4,3,2,1,0:T(8,128)}, f32[3,4,32,8,128]{4,3,2,1,0:T(8,128)S(1)}, u32[]{:S(2)}, u32[]{:S(2)}) collective-permute-start(f32[3,4,32,8,128]{4,3,2,1,0:T(8,128)} %get-tuple-element.25.refs_6_), channel_id=1, source_target_pairs={{0,1},{1,2},{2,3},{3,4},{4,5},{5,6},{6,7},{7,8},{8,9},{9,10},{10,1... | collective-permute-start | bytes 4718600 | tf_op jit(solution)/shard_map/ppermute | solution.py:361
  35.0 33.6 %collective-permute-start.6 = (f32[3,4,32,8,128]{4,3,2,1,0:T(8,128)}, f32[3,4,32,8,128]{4,3,2,1,0:T(8,128)S(1)}, u32[]{:S(2)}, u32[]{:S(2)}) collective-permute-start(f32[3,4,32,8,128]{4,3,2,1,0:T(8,128)} %get-tuple-element.28.refs_3_), channel_id=1, source_target_pairs={{0,15},{1,0},{2,1},{3,2},{4,3},{5,4},{6,5},{7,6},{8,7},{9,8},{10,9... | collective-permute-start | bytes 4718600 | tf_op jit(solution)/shard_map/ppermute | solution.py:362
  41.7 16.1 %copy-start.6 = (s32[4,256]{1,0:T(4,128)S(1)}, s32[4,256]{1,0:T(4,128)}, u32[]{:S(2)}) copy-start(s32[4,256]{1,0:T(4,128)} %param.16) | copy-start | bytes 12292
  41.7 16.1 %copy-start.7 = (s32[4,256]{1,0:T(4,128)S(1)}, s32[4,256]{1,0:T(4,128)}, u32[]{:S(2)}) copy-start(s32[4,256]{1,0:T(4,128)} %param.15) | copy-start | bytes 12292
  41.7 16.1 %copy-start.8 = (s32[256]{0:T(256)S(1)}, s32[256]{0:T(256)}, u32[]{:S(2)}) copy-start(s32[256]{0:T(256)} %param.14) | copy-start | bytes 3076
  41.8 16.1 %copy-start.9 = (s32[256]{0:T(256)S(1)}, s32[256]{0:T(256)}, u32[]{:S(2)}) copy-start(s32[256]{0:T(256)} %param.13) | copy-start | bytes 3076
  41.8 26.8 %copy-start.1 = (f32[4,256]{1,0:T(4,128)S(1)}, f32[4,256]{1,0:T(4,128)}, u32[]{:S(2)}) copy-start(f32[4,256]{1,0:T(4,128)} %obs_weight.1) | copy-start | bytes 12292
  55.7 7.4 %collective-permute-start.4 = (f32[4,3,8,1024]{3,2,1,0:T(8,128)S(1)}, f32[4,3,8,1024]{3,2,1,0:T(8,128)S(1)}, u32[]{:S(2)}, u32[]{:S(2)}) collective-permute-start(f32[4,3,8,1024]{3,2,1,0:T(8,128)S(1)} %get-tuple-element.31), channel_id=1, source_target_pairs={{0,15},{1,0},{2,1},{3,2},{4,3},{5,4},{6,5},{7,6},{8,7},{9,8},{10,9... | collective-permute-start | bytes 1179656 | tf_op jit(solution)/shard_map/ppermute | solution.py:369
  57.8 10.8 %collective-permute-start.3 = (f32[4,3,8,1024]{3,2,1,0:T(8,128)S(1)}, f32[4,3,8,1024]{3,2,1,0:T(8,128)S(1)}, u32[]{:S(2)}, u32[]{:S(2)}) collective-permute-start(f32[4,3,8,1024]{3,2,1,0:T(8,128)S(1)} %get-tuple-element.32), channel_id=1, source_target_pairs={{0,1},{1,2},{2,3},{3,4},{4,5},{5,6},{6,7},{7,8},{8,9},{9,10},{10,1... | collective-permute-start | bytes 1179656 | tf_op jit(solution)/shard_map/ppermute | solution.py:368
  102.4 11.5 %copy-start = (f32[4,2,8,128]{3,2,1,0:T(8,128)}, f32[4,2,8,128]{3,2,1,0:T(8,128)S(1)}, u32[]{:S(2)}) copy-start(f32[4,2,8,128]{3,2,1,0:T(8,128)S(1)} %model.1.own) | copy-start | bytes 98308
  102.4 31.4 %copy-start.3 = (f32[64]{0:T(128)S(1)}, f32[64]{0:T(128)}, u32[]{:S(2)}) copy-start(f32[64]{0:T(128)} %weights.1) | copy-start | bytes 772
  116.0 1.4 %collective-permute-start.7 = (f32[64,128]{1,0:T(8,128)}, f32[64,128]{1,0:T(8,128)S(1)}, u32[]{:S(2)}, u32[]{:S(2)}) collective-permute-start(f32[64,128]{1,0:T(8,128)} %get-tuple-element.30), channel_id=1, source_target_pairs={{0,1},{1,0},{2,3},{3,2},{4,5},{5,4},{6,7},{7,6},{8,9},{9,8},{10,11... | collective-permute-start | bytes 98312 | tf_op jit(solution)/shard_map/ppermute | solution.py:377
  118.2 3.9 %collective-permute-start.8 = (f32[64,128]{1,0:T(8,128)S(1)}, f32[64,128]{1,0:T(8,128)S(1)}, u32[]{:S(2)}, u32[]{:S(2)}) collective-permute-start(f32[64,128]{1,0:T(8,128)S(1)} %add.64), channel_id=1, source_target_pairs={{0,2},{1,3},{2,0},{3,1},{4,6},{5,7},{6,4},{7,5},{8,10},{9,11},{10,... | collective-permute-start | bytes 98312 | tf_op jit(solution)/shard_map/ppermute | solution.py:377
  122.1 5.4 %collective-permute-start.9 = (f32[64,128]{1,0:T(8,128)S(1)}, f32[64,128]{1,0:T(8,128)S(1)}, u32[]{:S(2)}, u32[]{:S(2)}) collective-permute-start(f32[64,128]{1,0:T(8,128)S(1)} %add.65), channel_id=1, source_target_pairs={{0,4},{1,5},{2,6},{3,7},{4,0},{5,1},{6,2},{7,3},{8,12},{9,13},{10,... | collective-permute-start | bytes 98312 | tf_op jit(solution)/shard_map/ppermute | solution.py:377
  127.6 5.4 %collective-permute-start.10 = (f32[64,128]{1,0:T(8,128)S(1)}, f32[64,128]{1,0:T(8,128)S(1)}, u32[]{:S(2)}, u32[]{:S(2)}) collective-permute-start(f32[64,128]{1,0:T(8,128)S(1)} %add.66), channel_id=1, source_target_pairs={{0,8},{1,9},{2,10},{3,11},{4,12},{5,13},{6,14},{7,15},{8,0},{9,1},... | collective-permute-start | bytes 98312 | tf_op jit(solution)/shard_map/ppermute | solution.py:377

commit v4 on v3

--- a/solution.py
+++ b/solution.py
@@ -94,7 +94,7 @@
 
 
 def model_kernel(
-    spots, turns, low_c, centre, high_c, obs_weight, *refs
+    spots, lanes, low_c, centre, high_c, obs_weight, *refs
 ):
     *sources, out, state, heights, spare, sems = refs
     tall, tiles = state.shape[1], state.shape[2]
@@ -236,32 +236,30 @@
             lax.fori_loop(0, (tall - 2 * low_row - 2) // ROWS, momentum_body, 0)
         h = fresh
 
-    points = obs_weight.shape[0]
-    stations = obs_weight.shape[1]
+    points, stations = spots.shape
     for group in range(stations // LANES):
 
         def pick(s, held):
             here = lane == s
-            fresh_held = list(held)
+            totals = [None] * STEPS
             for k in range(points):
                 spot = spots[k, group * LANES + s]
-                turn = turns[k, group * LANES + s]
+                row, tile = HALO + lax.shift_right_logical(spot, tiles.bit_length() - 1), spot & (tiles - 1)
+                factor = jnp.where(lane == lanes[k, group * LANES + s], obs_weight[k, group * LANES + s], 0.0)
                 for step in range(STEPS):
-                    value = pltpu.roll(heights[step, HALO + lax.shift_right_logical(spot, tiles.bit_length() - 1), spot & (tiles - 1)], turn, 1)
-                    fresh_held[step * points + k] = jnp.where(here, value, held[step * points + k])
-            return tuple(fresh_held)
+                    value = factor * heights[step, row, tile]
+                    totals[step] = value if totals[step] is None else totals[step] + value
+            return tuple(
+                jnp.where(here, jnp.sum(totals[step], axis=1, keepdims=True), held[step]) for step in range(STEPS)
+            )
 
         zero = jnp.zeros((8, LANES), jnp.float32)
-        held = lax.fori_loop(0, LANES, pick, (zero,) * (STEPS * points), unroll=16)
+        held = lax.fori_loop(0, LANES, pick, (zero,) * STEPS, unroll=32)
         for step in range(STEPS):
-            total = None
-            for k in range(points):
-                term = obs_weight[pl.ds(k, 1), pl.ds(group * LANES, LANES)] * held[step * points + k]
-                total = term if total is None else total + term
-            out[step, group] = total
-
-
-def run_model(spots, turns, low_c, centre, high_c, obs_weight, *parts):
+            out[step, group] = held[step]
+
+
+def run_model(spots, lanes, low_c, centre, high_c, obs_weight, *parts):
     fields, _, tiles, members, _ = parts[0].shape
     tall = sum(part.shape[1] for part in parts)
     smem = pl.BlockSpec(memory_space=pltpu.SMEM)
@@ -269,7 +267,7 @@
     groups = obs_weight.shape[1] // LANES
     return pl.pallas_call(
         model_kernel,
-        in_specs=[smem, smem] + [vmem] * 4 + [pl.BlockSpec(memory_space=pl.ANY)] * len(parts),
+        in_specs=[smem, smem, vmem, vmem, vmem, smem] + [pl.BlockSpec(memory_space=pl.ANY)] * len(parts),
         out_specs=vmem,
         out_shape=jax.ShapeDtypeStruct((STEPS, groups, members, LANES), jnp.float32),
         scratch_shapes=[
@@ -280,14 +278,14 @@
         ],
         compiler_params=pltpu.CompilerParams(vmem_limit_bytes=VMEM_MODEL),
         name="model",
-    )(spots, turns, low_c, centre, high_c, obs_weight, *parts)
+    )(spots, lanes, low_c, centre, high_c, obs_weight, *parts)
 
 
 def statistics_kernel(every, own, value, var, anom, packed):
     sources, steps, groups, members, _ = every.shape
     total = sources * members
     gram = jnp.zeros((total, total), jnp.float32)
-    pull = jnp.zeros((total, 1), jnp.float32)
+    pull = jnp.zeros((1, total), jnp.float32)
     for step in range(steps):
         for group in range(groups):
             at = pl.ds(group * LANES, LANES)
@@ -296,17 +294,21 @@
             anom[:, step, at] = (own[step, group] - mean) / perturb
             flat = (y - mean) / perturb
             weighted = flat * (1.0 / var[pl.ds(step, 1), at])
-            gram = gram + lax.dot_general(
-                weighted,
-                flat,
-                (((1,), (1,)), ((), ())),
-                precision=lax.Precision.HIGHEST,
-                preferred_element_type=jnp.float32,
-            )
             innov = value[pl.ds(step, 1), at] - mean
-            pull = pull + jnp.sum(weighted * innov, axis=1, keepdims=True)
-    packed[:, pl.ds(0, total)] = gram
-    packed[:, pl.ds(total, LANES - total)] = jnp.broadcast_to(pull, (total, LANES - total))
+            gram = gram + across(weighted, flat)
+            pull = pull + across(innov, weighted)
+    packed[pl.ds(0, total)] = gram
+    packed[pl.ds(total, 8)] = jnp.broadcast_to(pull, (8, total))
+
+
+def across(left, right):
+    return lax.dot_general(
+        left,
+        right,
+        (((1,), (1,)), ((), ())),
+        precision=lax.Precision.HIGHEST,
+        preferred_element_type=jnp.float32,
+    )
 
 
 def statistics(every, own, value, var):
@@ -315,7 +317,7 @@
         statistics_kernel,
         out_shape=[
             jax.ShapeDtypeStruct((members, steps, groups * LANES), jnp.float32),
-            jax.ShapeDtypeStruct((sources * members, LANES), jnp.float32),
+            jax.ShapeDtypeStruct((sources * members + 8, sources * members), jnp.float32),
         ],
         name="statistics",
     )(every, own, value, var)
@@ -342,10 +344,9 @@
 
     col = (station_col[None, :] + stencil_col) % columns
     spots = (station_row[None, :] + stencil_row) * (columns // LANES) + col // LANES
-    slot = jnp.arange(col.shape[1], dtype=jnp.int32)[None, :]
-    turns = (slot - col) % LANES
-
-    top, top_more, middle, bottom, bottom_more, partial_sum = prepare(place.reshape(1), weights, in_hbm(anomalies))
+    lanes = col % LANES
+
+    top, top_more, middle, bottom, bottom_more, partial_sum = prepare(place.reshape(1), in_hbm(weights), in_hbm(anomalies))
     own = [in_hbm(part) for part in (top, top_more, middle, bottom, bottom_more)]
     low = lax.ppermute(bottom, "sp", ring("sp", 1))
     high = lax.ppermute(top, "sp", ring("sp", -1))
@@ -368,7 +369,7 @@
     low_c = lax.ppermute(centre[:, :, rows - edge :], "sp", ring("sp", 1))
     high_c = lax.ppermute(centre[:, :, :edge], "sp", ring("sp", -1))
 
-    seen = run_model(spots, turns, low_c, centre, high_c, obs_weight, in_hbm(low), low_more, *own, in_hbm(high), high_more)
+    seen = run_model(spots, lanes, low_c, centre, high_c, obs_weight, in_hbm(low), low_more, *own, in_hbm(high), high_more)
     every = lax.all_to_all(jnp.broadcast_to(seen[None], (count, *seen.shape)), "mem", 0, 0, tiled=True)
     obs_anom, packed = statistics(every, seen, obs_value, obs_var)
     count = lax.axis_size("sp")
@@ -376,8 +377,8 @@
     while hop < count:
         packed = packed + lax.ppermute(packed, "sp", [(i, i ^ hop) for i in range(count)])
         hop *= 2
-    hessian = packed[:, :total] + (total - 1) * jnp.eye(total, dtype=jnp.float32)
-    gradient = (total - 1) * weights - packed[:, total]
+    hessian = packed[:total] + (total - 1) * jnp.eye(total, dtype=jnp.float32)
+    gradient = (total - 1) * weights - packed[total]
     return (obs_anom, gradient, hessian)
 
 

time: 135 us -> 133 us (0.985)
    pallas_call x1, Pallas kernels: 33.8 us -> 32.3 us  [run_model(): pl.pallas_call(model_kernel, in_specs=[smem, smem, vmem, vmem, vmem, smem...]
where the time goes in v4:
time: 133 us
  Pallas kernels  43 us (32%)
  blocking collectives  39.1 us (29%)
  waiting for transfers between devices  27.8 us (21%)
  starting transfers between devices  18.7 us (14%)
  other arithmetic  2.97 us (2%)
    pallas_call x1, Pallas kernels, run_model(): pl.pallas_call(model_kernel, in_specs=[smem, smem, vmem, vmem, vmem, smem...  32.3 us
    all_to_all x1, blocking collectives, body(): lax.all_to_all(jnp.broadcast_to(piece[None], (NEAR, *piece.shape)), 'mem'...  13.9 us
    all_to_all x1, blocking collectives, body(): lax.all_to_all(partial_sum, 'mem', 0, 0, axis_index_groups=near, tiled=True)  13.7 us
    ppermute x4, waiting for transfers between devices, body(): lax.ppermute(packed, 'sp', [(i, i ^ hop) for i in range(count)])  12.9 us
    all_to_all x1, blocking collectives, body(): lax.all_to_all(jnp.broadcast_to(seen[None], (count, *seen.shape)), 'mem',...  11.4 us
    pallas_call x1, Pallas kernels, prepare(): pl.pallas_call(prepare_kernel, grid=(fields, 2), in_specs=[smem, smem, pl...  8.16 us
    ppermute x1, starting transfers between devices, body(): high_more = lax.ppermute(top_more, 'sp', ring('sp', -1))  5.71 us
    ppermute x1, starting transfers between devices, body(): high = lax.ppermute(top, 'sp', ring('sp', -1))  5.61 us
  transfers between devices with their start and end apart: 11, of which 8 were waited for; matrix products, arithmetic and copies ran while one was open for 1% of the time, Pallas kernels for 0%

profile of v4, /device:TPU:0, one launch (start us, length us, event | category | flops | bytes accessed | tf_op | source)
XLA Modules:
  0.0 132.6 jit_solution(12835906369200844326)
XLA Ops:
  0.6 8.2 %prepare.1 = (f32[3,3,32,8,128]{4,3,2,1,0:T(8,128)}, f32[3,4,32,8,128]{4,3,2,1,0:T(8,128)}, f32[3,2,32,8,128]{4,3,2,1,0:T(8,128)}, f32[3,3,32,8,128]{4,3,2,1,0:T...) custom-call(s32[1]{0:T(128)} %bitcast.place, f32[64]{0:T(128)} %weights.1, f32[8,3,16,4096]{3,2,1,0:T(8,128)} %anom.1), custom_call_target="tpu_custom_call" | custom-call | tf_op jit(solution)/shard_map/prepare/pallas_call | solution.py:79
  8.8 5.6 %collective-permute-start.1 = (f32[3,3,32,8,128]{4,3,2,1,0:T(8,128)}, f32[3,3,32,8,128]{4,3,2,1,0:T(8,128)S(1)}, u32[]{:S(2)}, u32[]{:S(2)}) collective-permute-start(f32[3,3,32,8,128]{4,3,2,1,0:T(8,128)} %get-tuple-element.19.refs_2_), channel_id=1, source_target_pairs={{0,15},{1,0},{2,1},{3,2},{4,3},{5,4},{6,5},{7,6},{8,7},{9,8},{10,9... | collective-permute-start | bytes 3538952 | tf_op jit(solution)/shard_map/ppermute | solution.py:352
  14.4 13.7 %all_to_all.15 = f32[4,3,16,1024]{3,2,1,0:T(8,128)S(1)} all-to-all(f32[4,3,16,1024]{3,2,1,0:T(8,128)S(1)} %get-tuple-element.17), channel_id=1, replica_groups={{0,16,32,48},{64,80,96,112},{1,17,33,49},{65,81,97,113},{2,18,34,50},{6..., dimensions={0} | all-to-all | bytes 1572864 | tf_op jit(solution)/shard_map/all_to_all | solution.py:354
  28.2 0.3 collective-permute-done.refs_0_
  28.5 1.8 %collective-permute-start.2 = (f32[3,16,1024]{2,1,0:T(8,128)S(1)}, f32[3,16,1024]{2,1,0:T(8,128)S(1)}, u32[]{:S(2)}, u32[]{:S(2)}) collective-permute-start(f32[3,16,1024]{2,1,0:T(8,128)S(1)} %reduce_sum.9), channel_id=1, source_target_pairs={{0,64},{16,80},{32,96},{48,112},{64,0},{80,16},{96,32},{112,48},{1... | collective-permute-start | bytes 589832 | tf_op jit(solution)/shard_map/ppermute | solution.py:359
  30.3 3.9 %collective-permute-done.2 = f32[3,16,1024]{2,1,0:T(8,128)S(1)} collective-permute-done((f32[3,16,1024]{2,1,0:T(8,128)S(1)}, f32[3,16,1024]{2,1,0:T(8,128)S(1)}, u32[]{:S(2)}, u32[]{:S(2)}) %collective-permute-start.2) | collective-permute-done | bytes 196640 | tf_op jit(solution)/shard_map/ppermute | solution.py:359
  34.3 0.1 collective-permute-start.5
  34.4 5.7 %collective-permute-start.6 = (f32[3,4,32,8,128]{4,3,2,1,0:T(8,128)}, f32[3,4,32,8,128]{4,3,2,1,0:T(8,128)S(1)}, u32[]{:S(2)}, u32[]{:S(2)}) collective-permute-start(f32[3,4,32,8,128]{4,3,2,1,0:T(8,128)} %get-tuple-element.28.refs_3_), channel_id=1, source_target_pairs={{0,15},{1,0},{2,1},{3,2},{4,3},{5,4},{6,5},{7,6},{8,7},{9,8},{10,9... | collective-permute-start | bytes 4718600 | tf_op jit(solution)/shard_map/ppermute | solution.py:363
  40.1 0.9 dynamic-slice_add_fusion
  41.0 0.1 broadcast_in_dim.4
  41.1 0.0 copy-start.4
  41.1 0.0 copy-start.5
  41.1 0.0 copy-start.6
  41.1 0.0 copy-start.7
  41.2 0.0 copy-start.1
  41.2 13.9 %all_to_all.16.centre = f32[4,3,16,1024]{3,2,1,0:T(8,128)S(1)} all-to-all(f32[4,3,16,1024]{3,2,1,0:T(8,128)S(1)} %broadcast_in_dim.4), channel_id=1, replica_groups={{0,16,32,48},{64,80,96,112},{1,17,33,49},{65,81,97,113},{2,18,34,50},{6..., dimensions={0} | all-to-all | bytes 1572864 | tf_op jit(solution)/shard_map/all_to_all | solution.py:365
  55.0 0.1 fusion.4
  55.1 2.1 %collective-permute-start.4 = (f32[4,3,8,1024]{3,2,1,0:T(8,128)S(1)}, f32[4,3,8,1024]{3,2,1,0:T(8,128)S(1)}, u32[]{:S(2)}, u32[]{:S(2)}) collective-permute-start(f32[4,3,8,1024]{3,2,1,0:T(8,128)S(1)} %get-tuple-element.31), channel_id=1, source_target_pairs={{0,15},{1,0},{2,1},{3,2},{4,3},{5,4},{6,5},{7,6},{8,7},{9,8},{10,9... | collective-permute-start | bytes 1179656 | tf_op jit(solution)/shard_map/ppermute | solution.py:370
  57.2 5.2 %collective-permute-done.4.high_c = f32[4,3,8,1024]{3,2,1,0:T(8,128)S(1)} collective-permute-done((f32[4,3,8,1024]{3,2,1,0:T(8,128)S(1)}, f32[4,3,8,1024]{3,2,1,0:T(8,128)S(1)}, u32[]{:S(2)}, u32[]{:S(2)}) %collective-permute-start.4) | collective-permute-done | bytes 393248 | tf_op jit(solution)/shard_map/ppermute | solution.py:370
  62.5 5.5 %collective-permute-done.3.low_c = f32[4,3,8,1024]{3,2,1,0:T(8,128)S(1)} collective-permute-done((f32[4,3,8,1024]{3,2,1,0:T(8,128)S(1)}, f32[4,3,8,1024]{3,2,1,0:T(8,128)S(1)}, u32[]{:S(2)}, u32[]{:S(2)}) %collective-permute-start.3) | collective-permute-done | bytes 393248 | tf_op jit(solution)/shard_map/ppermute | solution.py:369
  68.0 0.0 copy-start.8
  68.0 32.3 %model.1.own = f32[4,2,8,128]{3,2,1,0:T(8,128)S(1)} custom-call(s32[4,256]{1,0:T(4,128)S(1)} %get-tuple-element.34.spots, s32[4,256]{1,0:T(4,128)S(1)} %get-tuple-element.33.lanes, f32[4,3,8,1024]{3,2,1,0:T(8,128)S(1)} %collective-permute-done.3.low_c, f32[4,3,16,1024]{3,2,1,0:T(8,128)S(1)} %all_to_all.16.centre, ...), custom_call_target="tpu_custom_call" | custom-call | tf_op jit(solution)/shard_map/model/pallas_call | solution.py:268
  100.4 11.4 %all_to_all.17.every = f32[8,4,2,8,128]{4,3,2,1,0:T(8,128)} all-to-all(f32[8,4,2,8,128]{4,3,2,1,0:T(8,128)S(1)} %broadcast_in_dim.5), channel_id=1, replica_groups=mesh['mem'=8,'sp'=16] {'mem'}, dimensions={0} | all-to-all | bytes 524288 | tf_op jit(solution)/shard_map/all_to_all | solution.py:373
  111.8 2.5 %statistics.1 = (f32[8,4,256]{2,1,0:T(4,128)}, f32[72,64]{1,0:T(8,128)}) custom-call(f32[8,4,2,8,128]{4,3,2,1,0:T(8,128)} %all_to_all.17.every, f32[4,2,8,128]{3,2,1,0:T(8,128)} %copy-done, f32[4,256]{1,0:T(4,128)} %value.1, f32[4,256]{1,0:T(4,128)} %var.1), custom_call_target="tpu_custom_call" | custom-call | tf_op jit(solution)/shard_map/statistics/pallas_call | solution.py:316
  114.3 1.4 %collective-permute-done.7 = f32[72,64]{1,0:T(8,128)S(1)} collective-permute-done((f32[72,64]{1,0:T(8,128)}, f32[72,64]{1,0:T(8,128)S(1)}, u32[]{:S(2)}, u32[]{:S(2)}) %collective-permute-start.7) | collective-permute-done | bytes 18464 | tf_op jit(solution)/shard_map/ppermute | solution.py:378
  115.7 0.8 add.64
  116.5 4.0 %collective-permute-done.8 = f32[72,64]{1,0:T(8,128)S(1)} collective-permute-done((f32[72,64]{1,0:T(8,128)S(1)}, f32[72,64]{1,0:T(8,128)S(1)}, u32[]{:S(2)}, u32[]{:S(2)}) %collective-permute-start.8) | collective-permute-done | bytes 18464 | tf_op jit(solution)/shard_map/ppermute | solution.py:378
  120.5 5.5 %collective-permute-done.9 = f32[72,64]{1,0:T(8,128)S(1)} collective-permute-done((f32[72,64]{1,0:T(8,128)S(1)}, f32[72,64]{1,0:T(8,128)S(1)}, u32[]{:S(2)}, u32[]{:S(2)}) %collective-permute-start.9) | collective-permute-done | bytes 18464 | tf_op jit(solution)/shard_map/ppermute | solution.py:378
  126.0 3.4 %collective-permute-start.10 = (f32[72,64]{1,0:T(8,128)S(1)}, f32[72,64]{1,0:T(8,128)S(1)}, u32[]{:S(2)}, u32[]{:S(2)}) collective-permute-start(f32[72,64]{1,0:T(8,128)S(1)} %add.66), channel_id=1, source_target_pairs={{0,8},{1,9},{2,10},{3,11},{4,12},{5,13},{6,14},{7,15},{8,0},{9,1},... | collective-permute-start | bytes 55304 | tf_op jit(solution)/shard_map/ppermute | solution.py:378
  129.4 2.0 %collective-permute-done.10 = f32[72,64]{1,0:T(8,128)S(1)} collective-permute-done((f32[72,64]{1,0:T(8,128)S(1)}, f32[72,64]{1,0:T(8,128)S(1)}, u32[]{:S(2)}, u32[]{:S(2)}) %collective-permute-start.10) | collective-permute-done | bytes 18464 | tf_op jit(solution)/shard_map/ppermute | solution.py:378
  131.4 0.5 fusion.3
  131.9 0.6 slice_add_fusion
  (27 shorter events, 0.2 us)
Async XLA Ops:
  8.8 19.7 %collective-permute-start = (f32[3,3,32,8,128]{4,3,2,1,0:T(8,128)}, f32[3,3,32,8,128]{4,3,2,1,0:T(8,128)S(1)}, u32[]{:S(2)}, u32[]{:S(2)}) collective-permute-start(f32[3,3,32,8,128]{4,3,2,1,0:T(8,128)} %get-tuple-element.18.refs_5_), channel_id=1, source_target_pairs={{0,1},{1,2},{2,3},{3,4},{4,5},{5,6},{6,7},{7,8},{8,9},{9,10},{10,1... | collective-permute-start | bytes 3538952 | tf_op jit(solution)/shard_map/ppermute | solution.py:351
  8.8 19.7 %collective-permute-start.1 = (f32[3,3,32,8,128]{4,3,2,1,0:T(8,128)}, f32[3,3,32,8,128]{4,3,2,1,0:T(8,128)S(1)}, u32[]{:S(2)}, u32[]{:S(2)}) collective-permute-start(f32[3,3,32,8,128]{4,3,2,1,0:T(8,128)} %get-tuple-element.19.refs_2_), channel_id=1, source_target_pairs={{0,15},{1,0},{2,1},{3,2},{4,3},{5,4},{6,5},{7,6},{8,7},{9,8},{10,9... | collective-permute-start | bytes 3538952 | tf_op jit(solution)/shard_map/ppermute | solution.py:352
  28.5 5.8 %copy-start.2 = (f32[3,3,32,8,128]{4,3,2,1,0:T(8,128)}, f32[3,3,32,8,128]{4,3,2,1,0:T(8,128)S(1)}, u32[]{:S(2)}) copy-start(f32[3,3,32,8,128]{4,3,2,1,0:T(8,128)S(1)} %collective-permute-done.refs_0_) | copy-start | bytes 3538948
  28.5 5.8 %copy-start.3 = (f32[3,3,32,8,128]{4,3,2,1,0:T(8,128)}, f32[3,3,32,8,128]{4,3,2,1,0:T(8,128)S(1)}, u32[]{:S(2)}) copy-start(f32[3,3,32,8,128]{4,3,2,1,0:T(8,128)S(1)} %collective-permute-done.1.refs_7_) | copy-start | bytes 3538948
  28.5 5.7 %collective-permute-start.2 = (f32[3,16,1024]{2,1,0:T(8,128)S(1)}, f32[3,16,1024]{2,1,0:T(8,128)S(1)}, u32[]{:S(2)}, u32[]{:S(2)}) collective-permute-start(f32[3,16,1024]{2,1,0:T(8,128)S(1)} %reduce_sum.9), channel_id=1, source_target_pairs={{0,64},{16,80},{32,96},{48,112},{64,0},{80,16},{96,32},{112,48},{1... | collective-permute-start | bytes 589832 | tf_op jit(solution)/shard_map/ppermute | solution.py:359
  34.3 33.7 %collective-permute-start.5 = (f32[3,4,32,8,128]{4,3,2,1,0:T(8,128)}, f32[3,4,32,8,128]{4,3,2,1,0:T(8,128)S(1)}, u32[]{:S(2)}, u32[]{:S(2)}) collective-permute-start(f32[3,4,32,8,128]{4,3,2,1,0:T(8,128)} %get-tuple-element.25.refs_6_), channel_id=1, source_target_pairs={{0,1},{1,2},{2,3},{3,4},{4,5},{5,6},{6,7},{7,8},{8,9},{9,10},{10,1... | collective-permute-start | bytes 4718600 | tf_op jit(solution)/shard_map/ppermute | solution.py:362
  34.4 33.6 %collective-permute-start.6 = (f32[3,4,32,8,128]{4,3,2,1,0:T(8,128)}, f32[3,4,32,8,128]{4,3,2,1,0:T(8,128)S(1)}, u32[]{:S(2)}, u32[]{:S(2)}) collective-permute-start(f32[3,4,32,8,128]{4,3,2,1,0:T(8,128)} %get-tuple-element.28.refs_3_), channel_id=1, source_target_pairs={{0,15},{1,0},{2,1},{3,2},{4,3},{5,4},{6,5},{7,6},{8,7},{9,8},{10,9... | collective-permute-start | bytes 4718600 | tf_op jit(solution)/shard_map/ppermute | solution.py:363
  41.1 16.1 %copy-start.4 = (s32[4,256]{1,0:T(4,128)S(1)}, s32[4,256]{1,0:T(4,128)}, u32[]{:S(2)}) copy-start(s32[4,256]{1,0:T(4,128)} %param.16) | copy-start | bytes 12292
  41.1 16.1 %copy-start.5 = (s32[4,256]{1,0:T(4,128)S(1)}, s32[4,256]{1,0:T(4,128)}, u32[]{:S(2)}) copy-start(s32[4,256]{1,0:T(4,128)} %param.15) | copy-start | bytes 12292
  41.1 16.1 %copy-start.6 = (s32[256]{0:T(256)S(1)}, s32[256]{0:T(256)}, u32[]{:S(2)}) copy-start(s32[256]{0:T(256)} %param.14) | copy-start | bytes 3076
  41.1 16.1 %copy-start.7 = (s32[256]{0:T(256)S(1)}, s32[256]{0:T(256)}, u32[]{:S(2)}) copy-start(s32[256]{0:T(256)} %param.13) | copy-start | bytes 3076
  41.2 26.8 %copy-start.1 = (f32[4,256]{1,0:T(4,128)S(1)}, f32[4,256]{1,0:T(4,128)}, u32[]{:S(2)}) copy-start(f32[4,256]{1,0:T(4,128)} %obs_weight.1) | copy-start | bytes 12292
  55.1 7.4 %collective-permute-start.4 = (f32[4,3,8,1024]{3,2,1,0:T(8,128)S(1)}, f32[4,3,8,1024]{3,2,1,0:T(8,128)S(1)}, u32[]{:S(2)}, u32[]{:S(2)}) collective-permute-start(f32[4,3,8,1024]{3,2,1,0:T(8,128)S(1)} %get-tuple-element.31), channel_id=1, source_target_pairs={{0,15},{1,0},{2,1},{3,2},{4,3},{5,4},{6,5},{7,6},{8,7},{9,8},{10,9... | collective-permute-start | bytes 1179656 | tf_op jit(solution)/shard_map/ppermute | solution.py:370
  57.2 10.8 %collective-permute-start.3 = (f32[4,3,8,1024]{3,2,1,0:T(8,128)S(1)}, f32[4,3,8,1024]{3,2,1,0:T(8,128)S(1)}, u32[]{:S(2)}, u32[]{:S(2)}) collective-permute-start(f32[4,3,8,1024]{3,2,1,0:T(8,128)S(1)} %get-tuple-element.32), channel_id=1, source_target_pairs={{0,1},{1,2},{2,3},{3,4},{4,5},{5,6},{6,7},{7,8},{8,9},{9,10},{10,1... | collective-permute-start | bytes 1179656 | tf_op jit(solution)/shard_map/ppermute | solution.py:369
  68.0 63.4 %copy-start.8 = (f32[64]{0:T(128)S(1)}, f32[64]{0:T(128)}, u32[]{:S(2)}) copy-start(f32[64]{0:T(128)} %weights.1) | copy-start | bytes 772
  100.3 11.5 %copy-start = (f32[4,2,8,128]{3,2,1,0:T(8,128)}, f32[4,2,8,128]{3,2,1,0:T(8,128)S(1)}, u32[]{:S(2)}) copy-start(f32[4,2,8,128]{3,2,1,0:T(8,128)S(1)} %model.1.own) | copy-start | bytes 98308
  114.3 1.4 %collective-permute-start.7 = (f32[72,64]{1,0:T(8,128)}, f32[72,64]{1,0:T(8,128)S(1)}, u32[]{:S(2)}, u32[]{:S(2)}) collective-permute-start(f32[72,64]{1,0:T(8,128)} %get-tuple-element.30), channel_id=1, source_target_pairs={{0,1},{1,0},{2,3},{3,2},{4,5},{5,4},{6,7},{7,6},{8,9},{9,8},{10,11... | collective-permute-start | bytes 55304 | tf_op jit(solution)/shard_map/ppermute | solution.py:378
  116.5 4.0 %collective-permute-start.8 = (f32[72,64]{1,0:T(8,128)S(1)}, f32[72,64]{1,0:T(8,128)S(1)}, u32[]{:S(2)}, u32[]{:S(2)}) collective-permute-start(f32[72,64]{1,0:T(8,128)S(1)} %add.64), channel_id=1, source_target_pairs={{0,2},{1,3},{2,0},{3,1},{4,6},{5,7},{6,4},{7,5},{8,10},{9,11},{10,... | collective-permute-start | bytes 55304 | tf_op jit(solution)/shard_map/ppermute | solution.py:378
  120.5 5.5 %collective-permute-start.9 = (f32[72,64]{1,0:T(8,128)S(1)}, f32[72,64]{1,0:T(8,128)S(1)}, u32[]{:S(2)}, u32[]{:S(2)}) collective-permute-start(f32[72,64]{1,0:T(8,128)S(1)} %add.65), channel_id=1, source_target_pairs={{0,4},{1,5},{2,6},{3,7},{4,0},{5,1},{6,2},{7,3},{8,12},{9,13},{10,... | collective-permute-start | bytes 55304 | tf_op jit(solution)/shard_map/ppermute | solution.py:378
  126.0 5.5 %collective-permute-start.10 = (f32[72,64]{1,0:T(8,128)S(1)}, f32[72,64]{1,0:T(8,128)S(1)}, u32[]{:S(2)}, u32[]{:S(2)}) collective-permute-start(f32[72,64]{1,0:T(8,128)S(1)} %add.66), channel_id=1, source_target_pairs={{0,8},{1,9},{2,10},{3,11},{4,12},{5,13},{6,14},{7,15},{8,0},{9,1},... | collective-permute-start | bytes 55304 | tf_op jit(solution)/shard_map/ppermute | solution.py:378

commit v5 on v4

--- a/solution.py
+++ b/solution.py
@@ -34,18 +34,18 @@
 
 def prepare_kernel(place, weights, anom, *outs):
     *parts, partial = outs
-    members, half = anom.shape[0], anom.shape[2]
+    members, half = anom.shape[0], anom.shape[2] // 2
     chunks, width = partial.shape[0], partial.shape[3]
     first = place[0] * members
     scales = [weights[first + m] for m in range(members)]
     per = width // (SPAN * LANES)
     homes = [(part, r) for part in parts for r in range(part.shape[1])]
 
-    def turn(homes):
+    def turn(homes, above):
         def columns(c, carry):
             swapped, totals = [], []
             for i in range(SPAN):
-                block = anom[:, 0, :, pl.ds(pl.multiple_of((c * SPAN + i) * LANES, LANES), LANES)]
+                block = anom[:, 0, pl.ds(above, half), pl.ds(pl.multiple_of((c * SPAN + i) * LANES, LANES), LANES)]
                 swapped.append(jnp.swapaxes(block, 0, 1))
                 total = scales[0] * block[0]
                 for m in range(1, members):
@@ -55,21 +55,17 @@
             for i in range(SPAN):
                 for r, (part, home) in enumerate(homes):
                     part[0, home, c * SPAN + i] = swapped[i][r]
-                partial[lax.div(c, per), 0, :, pl.ds(inner + i * LANES, LANES)] = totals[i]
+                partial[lax.div(c, per), 0, pl.ds(above, half), pl.ds(inner + i * LANES, LANES)] = totals[i]
             return carry
 
         lax.fori_loop(0, chunks * per, columns, 0)
 
-    for step in range(2):
-
-        @pl.when(pl.program_id(1) == step)
-        def _():
-            turn(homes[step * half : (step + 1) * half])
+    for above in (0, half):
+        turn(homes[above : above + half], above)
 
 
 def prepare(place, weights, anomalies):
     members, fields, rows, columns = anomalies.shape
-    half = rows // 2
     chunks = NEAR
     width = columns // chunks
     smem = pl.BlockSpec(memory_space=pltpu.SMEM)
@@ -78,11 +74,11 @@
     parts = (EARLY, late, rows - 2 * HALO, EARLY, late)
     return pl.pallas_call(
         prepare_kernel,
-        grid=(fields, 2),
-        in_specs=[smem, smem, pl.BlockSpec((members, 1, half, columns), lambda f, r: (0, f, r, 0))],
+        grid=(fields,),
+        in_specs=[smem, smem, pl.BlockSpec((members, 1, rows, columns), lambda f: (0, f, 0, 0))],
         out_specs=[
-            *(pl.BlockSpec((1, part, tiles, members, LANES), lambda f, r: (f, 0, 0, 0, 0)) for part in parts),
-            pl.BlockSpec((chunks, 1, half, width), lambda f, r: (0, f, r, 0)),
+            *(pl.BlockSpec((1, part, tiles, members, LANES), lambda f: (f, 0, 0, 0, 0)) for part in parts),
+            pl.BlockSpec((chunks, 1, rows, width), lambda f: (0, f, 0, 0)),
         ],
         out_shape=[
             *(pltpu.HBM((fields, part, tiles, members, LANES), jnp.float32) for part in parts),

time: 133 us -> 132 us (level)
  no operation moved by 1% of the time
where the time goes in v5:
time: 132 us
  Pallas kernels  42.2 us (32%)
  blocking collectives  39.1 us (30%)
  waiting for transfers between devices  27.8 us (21%)
  starting transfers between devices  18.7 us (14%)
  other arithmetic  2.97 us (2%)
    pallas_call x1, Pallas kernels, run_model(): pl.pallas_call(model_kernel, in_specs=[smem, smem, vmem, vmem, vmem, smem...  32.3 us
    all_to_all x1, blocking collectives, body(): lax.all_to_all(jnp.broadcast_to(piece[None], (NEAR, *piece.shape)), 'mem'...  13.9 us
    all_to_all x1, blocking collectives, body(): lax.all_to_all(partial_sum, 'mem', 0, 0, axis_index_groups=near, tiled=True)  13.7 us
    ppermute x4, waiting for transfers between devices, body(): lax.ppermute(packed, 'sp', [(i, i ^ hop) for i in range(count)])  12.9 us
    all_to_all x1, blocking collectives, body(): lax.all_to_all(jnp.broadcast_to(seen[None], (count, *seen.shape)), 'mem',...  11.4 us
    pallas_call x1, Pallas kernels, prepare(): pl.pallas_call(prepare_kernel, grid=(fields,), in_specs=[smem, smem, pl.B...  7.39 us
    ppermute x1, starting transfers between devices, body(): high_more = lax.ppermute(top_more, 'sp', ring('sp', -1))  5.71 us
    ppermute x1, starting transfers between devices, body(): high = lax.ppermute(top, 'sp', ring('sp', -1))  5.61 us
  transfers between devices with their start and end apart: 11, of which 8 were waited for; matrix products, arithmetic and copies ran while one was open for 1% of the time, Pallas kernels for 0%

profile of v5, /device:TPU:0, one launch (start us, length us, event | category | flops | bytes accessed | tf_op | source)
XLA Modules:
  0.0 131.8 jit_solution(1783743128346718664)
XLA Ops:
  0.6 7.4 %prepare.1 = (f32[3,3,32,8,128]{4,3,2,1,0:T(8,128)}, f32[3,4,32,8,128]{4,3,2,1,0:T(8,128)}, f32[3,2,32,8,128]{4,3,2,1,0:T(8,128)}, f32[3,3,32,8,128]{4,3,2,1,0:T...) custom-call(s32[1]{0:T(128)} %bitcast.place, f32[64]{0:T(128)} %weights.1, f32[8,3,16,4096]{3,2,1,0:T(8,128)} %anom.1), custom_call_target="tpu_custom_call" | custom-call | tf_op jit(solution)/shard_map/prepare/pallas_call | solution.py:75
  8.0 5.6 %collective-permute-start.1 = (f32[3,3,32,8,128]{4,3,2,1,0:T(8,128)}, f32[3,3,32,8,128]{4,3,2,1,0:T(8,128)S(1)}, u32[]{:S(2)}, u32[]{:S(2)}) collective-permute-start(f32[3,3,32,8,128]{4,3,2,1,0:T(8,128)} %get-tuple-element.19.refs_2_), channel_id=1, source_target_pairs={{0,15},{1,0},{2,1},{3,2},{4,3},{5,4},{6,5},{7,6},{8,7},{9,8},{10,9... | collective-permute-start | bytes 3538952 | tf_op jit(solution)/shard_map/ppermute | solution.py:348
  13.6 13.7 %all_to_all.15 = f32[4,3,16,1024]{3,2,1,0:T(8,128)S(1)} all-to-all(f32[4,3,16,1024]{3,2,1,0:T(8,128)S(1)} %get-tuple-element.17), channel_id=1, replica_groups={{0,16,32,48},{64,80,96,112},{1,17,33,49},{65,81,97,113},{2,18,34,50},{6..., dimensions={0} | all-to-all | bytes 1572864 | tf_op jit(solution)/shard_map/all_to_all | solution.py:350
  27.4 0.3 collective-permute-done.refs_0_
  27.7 1.8 %collective-permute-start.2 = (f32[3,16,1024]{2,1,0:T(8,128)S(1)}, f32[3,16,1024]{2,1,0:T(8,128)S(1)}, u32[]{:S(2)}, u32[]{:S(2)}) collective-permute-start(f32[3,16,1024]{2,1,0:T(8,128)S(1)} %reduce_sum.9), channel_id=1, source_target_pairs={{0,64},{16,80},{32,96},{48,112},{64,0},{80,16},{96,32},{112,48},{1... | collective-permute-start | bytes 589832 | tf_op jit(solution)/shard_map/ppermute | solution.py:355
  29.6 3.9 %collective-permute-done.2 = f32[3,16,1024]{2,1,0:T(8,128)S(1)} collective-permute-done((f32[3,16,1024]{2,1,0:T(8,128)S(1)}, f32[3,16,1024]{2,1,0:T(8,128)S(1)}, u32[]{:S(2)}, u32[]{:S(2)}) %collective-permute-start.2) | collective-permute-done | bytes 196640 | tf_op jit(solution)/shard_map/ppermute | solution.py:355
  33.5 0.1 collective-permute-start.5
  33.6 5.7 %collective-permute-start.6 = (f32[3,4,32,8,128]{4,3,2,1,0:T(8,128)}, f32[3,4,32,8,128]{4,3,2,1,0:T(8,128)S(1)}, u32[]{:S(2)}, u32[]{:S(2)}) collective-permute-start(f32[3,4,32,8,128]{4,3,2,1,0:T(8,128)} %get-tuple-element.28.refs_3_), channel_id=1, source_target_pairs={{0,15},{1,0},{2,1},{3,2},{4,3},{5,4},{6,5},{7,6},{8,7},{9,8},{10,9... | collective-permute-start | bytes 4718600 | tf_op jit(solution)/shard_map/ppermute | solution.py:359
  39.3 0.9 dynamic-slice_add_fusion
  40.3 0.1 broadcast_in_dim.4
  40.3 0.0 copy-start.4
  40.4 0.0 copy-start.5
  40.4 0.0 copy-start.6
  40.4 0.0 copy-start.7
  40.4 0.0 copy-start.1
  40.4 13.9 %all_to_all.16.centre = f32[4,3,16,1024]{3,2,1,0:T(8,128)S(1)} all-to-all(f32[4,3,16,1024]{3,2,1,0:T(8,128)S(1)} %broadcast_in_dim.4), channel_id=1, replica_groups={{0,16,32,48},{64,80,96,112},{1,17,33,49},{65,81,97,113},{2,18,34,50},{6..., dimensions={0} | all-to-all | bytes 1572864 | tf_op jit(solution)/shard_map/all_to_all | solution.py:361
  54.3 0.1 fusion.4
  54.3 2.1 %collective-permute-start.4 = (f32[4,3,8,1024]{3,2,1,0:T(8,128)S(1)}, f32[4,3,8,1024]{3,2,1,0:T(8,128)S(1)}, u32[]{:S(2)}, u32[]{:S(2)}) collective-permute-start(f32[4,3,8,1024]{3,2,1,0:T(8,128)S(1)} %get-tuple-element.31), channel_id=1, source_target_pairs={{0,15},{1,0},{2,1},{3,2},{4,3},{5,4},{6,5},{7,6},{8,7},{9,8},{10,9... | collective-permute-start | bytes 1179656 | tf_op jit(solution)/shard_map/ppermute | solution.py:366
  56.5 5.2 %collective-permute-done.4.high_c = f32[4,3,8,1024]{3,2,1,0:T(8,128)S(1)} collective-permute-done((f32[4,3,8,1024]{3,2,1,0:T(8,128)S(1)}, f32[4,3,8,1024]{3,2,1,0:T(8,128)S(1)}, u32[]{:S(2)}, u32[]{:S(2)}) %collective-permute-start.4) | collective-permute-done | bytes 393248 | tf_op jit(solution)/shard_map/ppermute | solution.py:366
  61.7 5.5 %collective-permute-done.3.low_c = f32[4,3,8,1024]{3,2,1,0:T(8,128)S(1)} collective-permute-done((f32[4,3,8,1024]{3,2,1,0:T(8,128)S(1)}, f32[4,3,8,1024]{3,2,1,0:T(8,128)S(1)}, u32[]{:S(2)}, u32[]{:S(2)}) %collective-permute-start.3) | collective-permute-done | bytes 393248 | tf_op jit(solution)/shard_map/ppermute | solution.py:365
  67.2 32.3 %model.1.own = f32[4,2,8,128]{3,2,1,0:T(8,128)S(1)} custom-call(s32[4,256]{1,0:T(4,128)S(1)} %get-tuple-element.34.spots, s32[4,256]{1,0:T(4,128)S(1)} %get-tuple-element.33.lanes, f32[4,3,8,1024]{3,2,1,0:T(8,128)S(1)} %collective-permute-done.3.low_c, f32[4,3,16,1024]{3,2,1,0:T(8,128)S(1)} %all_to_all.16.centre, ...), custom_call_target="tpu_custom_call" | custom-call | tf_op jit(solution)/shard_map/model/pallas_call | solution.py:264
  99.6 0.0 copy-start
  99.6 11.4 %all_to_all.17.every = f32[8,4,2,8,128]{4,3,2,1,0:T(8,128)} all-to-all(f32[8,4,2,8,128]{4,3,2,1,0:T(8,128)S(1)} %broadcast_in_dim.5), channel_id=1, replica_groups=mesh['mem'=8,'sp'=16] {'mem'}, dimensions={0} | all-to-all | bytes 524288 | tf_op jit(solution)/shard_map/all_to_all | solution.py:369
  111.0 2.5 %statistics.1 = (f32[8,4,256]{2,1,0:T(4,128)}, f32[72,64]{1,0:T(8,128)}) custom-call(f32[8,4,2,8,128]{4,3,2,1,0:T(8,128)} %all_to_all.17.every, f32[4,2,8,128]{3,2,1,0:T(8,128)} %copy-done, f32[4,256]{1,0:T(4,128)} %value.1, f32[4,256]{1,0:T(4,128)} %var.1), custom_call_target="tpu_custom_call" | custom-call | tf_op jit(solution)/shard_map/statistics/pallas_call | solution.py:312
  113.6 1.4 %collective-permute-done.7 = f32[72,64]{1,0:T(8,128)S(1)} collective-permute-done((f32[72,64]{1,0:T(8,128)}, f32[72,64]{1,0:T(8,128)S(1)}, u32[]{:S(2)}, u32[]{:S(2)}) %collective-permute-start.7) | collective-permute-done | bytes 18464 | tf_op jit(solution)/shard_map/ppermute | solution.py:374
  115.0 0.8 add.64
  115.8 4.0 %collective-permute-done.8 = f32[72,64]{1,0:T(8,128)S(1)} collective-permute-done((f32[72,64]{1,0:T(8,128)S(1)}, f32[72,64]{1,0:T(8,128)S(1)}, u32[]{:S(2)}, u32[]{:S(2)}) %collective-permute-start.8) | collective-permute-done | bytes 18464 | tf_op jit(solution)/shard_map/ppermute | solution.py:374
  119.7 5.5 %collective-permute-done.9 = f32[72,64]{1,0:T(8,128)S(1)} collective-permute-done((f32[72,64]{1,0:T(8,128)S(1)}, f32[72,64]{1,0:T(8,128)S(1)}, u32[]{:S(2)}, u32[]{:S(2)}) %collective-permute-start.9) | collective-permute-done | bytes 18464 | tf_op jit(solution)/shard_map/ppermute | solution.py:374
  125.2 3.4 %collective-permute-start.10 = (f32[72,64]{1,0:T(8,128)S(1)}, f32[72,64]{1,0:T(8,128)S(1)}, u32[]{:S(2)}, u32[]{:S(2)}) collective-permute-start(f32[72,64]{1,0:T(8,128)S(1)} %add.66), channel_id=1, source_target_pairs={{0,8},{1,9},{2,10},{3,11},{4,12},{5,13},{6,14},{7,15},{8,0},{9,1},... | collective-permute-start | bytes 55304 | tf_op jit(solution)/shard_map/ppermute | solution.py:374
  128.6 2.0 %collective-permute-done.10 = f32[72,64]{1,0:T(8,128)S(1)} collective-permute-done((f32[72,64]{1,0:T(8,128)S(1)}, f32[72,64]{1,0:T(8,128)S(1)}, u32[]{:S(2)}, u32[]{:S(2)}) %collective-permute-start.10) | collective-permute-done | bytes 18464 | tf_op jit(solution)/shard_map/ppermute | solution.py:374
  130.7 0.5 fusion.3
  131.2 0.6 slice_add_fusion
  (27 shorter events, 0.2 us)
Async XLA Ops:
  8.0 19.7 %collective-permute-start = (f32[3,3,32,8,128]{4,3,2,1,0:T(8,128)}, f32[3,3,32,8,128]{4,3,2,1,0:T(8,128)S(1)}, u32[]{:S(2)}, u32[]{:S(2)}) collective-permute-start(f32[3,3,32,8,128]{4,3,2,1,0:T(8,128)} %get-tuple-element.18.refs_5_), channel_id=1, source_target_pairs={{0,1},{1,2},{2,3},{3,4},{4,5},{5,6},{6,7},{7,8},{8,9},{9,10},{10,1... | collective-permute-start | bytes 3538952 | tf_op jit(solution)/shard_map/ppermute | solution.py:347
  8.0 19.7 %collective-permute-start.1 = (f32[3,3,32,8,128]{4,3,2,1,0:T(8,128)}, f32[3,3,32,8,128]{4,3,2,1,0:T(8,128)S(1)}, u32[]{:S(2)}, u32[]{:S(2)}) collective-permute-start(f32[3,3,32,8,128]{4,3,2,1,0:T(8,128)} %get-tuple-element.19.refs_2_), channel_id=1, source_target_pairs={{0,15},{1,0},{2,1},{3,2},{4,3},{5,4},{6,5},{7,6},{8,7},{9,8},{10,9... | collective-permute-start | bytes 3538952 | tf_op jit(solution)/shard_map/ppermute | solution.py:348
  27.7 5.8 %copy-start.2 = (f32[3,3,32,8,128]{4,3,2,1,0:T(8,128)}, f32[3,3,32,8,128]{4,3,2,1,0:T(8,128)S(1)}, u32[]{:S(2)}) copy-start(f32[3,3,32,8,128]{4,3,2,1,0:T(8,128)S(1)} %collective-permute-done.refs_0_) | copy-start | bytes 3538948
  27.7 5.8 %copy-start.3 = (f32[3,3,32,8,128]{4,3,2,1,0:T(8,128)}, f32[3,3,32,8,128]{4,3,2,1,0:T(8,128)S(1)}, u32[]{:S(2)}) copy-start(f32[3,3,32,8,128]{4,3,2,1,0:T(8,128)S(1)} %collective-permute-done.1.refs_7_) | copy-start | bytes 3538948
  27.7 5.7 %collective-permute-start.2 = (f32[3,16,1024]{2,1,0:T(8,128)S(1)}, f32[3,16,1024]{2,1,0:T(8,128)S(1)}, u32[]{:S(2)}, u32[]{:S(2)}) collective-permute-start(f32[3,16,1024]{2,1,0:T(8,128)S(1)} %reduce_sum.9), channel_id=1, source_target_pairs={{0,64},{16,80},{32,96},{48,112},{64,0},{80,16},{96,32},{112,48},{1... | collective-permute-start | bytes 589832 | tf_op jit(solution)/shard_map/ppermute | solution.py:355
  33.5 33.7 %collective-permute-start.5 = (f32[3,4,32,8,128]{4,3,2,1,0:T(8,128)}, f32[3,4,32,8,128]{4,3,2,1,0:T(8,128)S(1)}, u32[]{:S(2)}, u32[]{:S(2)}) collective-permute-start(f32[3,4,32,8,128]{4,3,2,1,0:T(8,128)} %get-tuple-element.25.refs_6_), channel_id=1, source_target_pairs={{0,1},{1,2},{2,3},{3,4},{4,5},{5,6},{6,7},{7,8},{8,9},{9,10},{10,1... | collective-permute-start | bytes 4718600 | tf_op jit(solution)/shard_map/ppermute | solution.py:358
  33.6 33.6 %collective-permute-start.6 = (f32[3,4,32,8,128]{4,3,2,1,0:T(8,128)}, f32[3,4,32,8,128]{4,3,2,1,0:T(8,128)S(1)}, u32[]{:S(2)}, u32[]{:S(2)}) collective-permute-start(f32[3,4,32,8,128]{4,3,2,1,0:T(8,128)} %get-tuple-element.28.refs_3_), channel_id=1, source_target_pairs={{0,15},{1,0},{2,1},{3,2},{4,3},{5,4},{6,5},{7,6},{8,7},{9,8},{10,9... | collective-permute-start | bytes 4718600 | tf_op jit(solution)/shard_map/ppermute | solution.py:359
  40.3 16.1 %copy-start.4 = (s32[4,256]{1,0:T(4,128)S(1)}, s32[4,256]{1,0:T(4,128)}, u32[]{:S(2)}) copy-start(s32[4,256]{1,0:T(4,128)} %param.16) | copy-start | bytes 12292
  40.4 16.1 %copy-start.5 = (s32[4,256]{1,0:T(4,128)S(1)}, s32[4,256]{1,0:T(4,128)}, u32[]{:S(2)}) copy-start(s32[4,256]{1,0:T(4,128)} %param.15) | copy-start | bytes 12292
  40.4 16.1 %copy-start.6 = (s32[256]{0:T(256)S(1)}, s32[256]{0:T(256)}, u32[]{:S(2)}) copy-start(s32[256]{0:T(256)} %param.14) | copy-start | bytes 3076
  40.4 16.1 %copy-start.7 = (s32[256]{0:T(256)S(1)}, s32[256]{0:T(256)}, u32[]{:S(2)}) copy-start(s32[256]{0:T(256)} %param.13) | copy-start | bytes 3076
  40.4 26.8 %copy-start.1 = (f32[4,256]{1,0:T(4,128)S(1)}, f32[4,256]{1,0:T(4,128)}, u32[]{:S(2)}) copy-start(f32[4,256]{1,0:T(4,128)} %obs_weight.1) | copy-start | bytes 12292
  54.3 7.4 %collective-permute-start.4 = (f32[4,3,8,1024]{3,2,1,0:T(8,128)S(1)}, f32[4,3,8,1024]{3,2,1,0:T(8,128)S(1)}, u32[]{:S(2)}, u32[]{:S(2)}) collective-permute-start(f32[4,3,8,1024]{3,2,1,0:T(8,128)S(1)} %get-tuple-element.31), channel_id=1, source_target_pairs={{0,15},{1,0},{2,1},{3,2},{4,3},{5,4},{6,5},{7,6},{8,7},{9,8},{10,9... | collective-permute-start | bytes 1179656 | tf_op jit(solution)/shard_map/ppermute | solution.py:366
  56.4 10.8 %collective-permute-start.3 = (f32[4,3,8,1024]{3,2,1,0:T(8,128)S(1)}, f32[4,3,8,1024]{3,2,1,0:T(8,128)S(1)}, u32[]{:S(2)}, u32[]{:S(2)}) collective-permute-start(f32[4,3,8,1024]{3,2,1,0:T(8,128)S(1)} %get-tuple-element.32), channel_id=1, source_target_pairs={{0,1},{1,2},{2,3},{3,4},{4,5},{5,6},{6,7},{7,8},{8,9},{9,10},{10,1... | collective-permute-start | bytes 1179656 | tf_op jit(solution)/shard_map/ppermute | solution.py:365
  67.2 63.4 %copy-start.8 = (f32[64]{0:T(128)S(1)}, f32[64]{0:T(128)}, u32[]{:S(2)}) copy-start(f32[64]{0:T(128)} %weights.1) | copy-start | bytes 772
  99.6 11.5 %copy-start = (f32[4,2,8,128]{3,2,1,0:T(8,128)}, f32[4,2,8,128]{3,2,1,0:T(8,128)S(1)}, u32[]{:S(2)}) copy-start(f32[4,2,8,128]{3,2,1,0:T(8,128)S(1)} %model.1.own) | copy-start | bytes 98308
  113.6 1.4 %collective-permute-start.7 = (f32[72,64]{1,0:T(8,128)}, f32[72,64]{1,0:T(8,128)S(1)}, u32[]{:S(2)}, u32[]{:S(2)}) collective-permute-start(f32[72,64]{1,0:T(8,128)} %get-tuple-element.30), channel_id=1, source_target_pairs={{0,1},{1,0},{2,3},{3,2},{4,5},{5,4},{6,7},{7,6},{8,9},{9,8},{10,11... | collective-permute-start | bytes 55304 | tf_op jit(solution)/shard_map/ppermute | solution.py:374
  115.8 4.0 %collective-permute-start.8 = (f32[72,64]{1,0:T(8,128)S(1)}, f32[72,64]{1,0:T(8,128)S(1)}, u32[]{:S(2)}, u32[]{:S(2)}) collective-permute-start(f32[72,64]{1,0:T(8,128)S(1)} %add.64), channel_id=1, source_target_pairs={{0,2},{1,3},{2,0},{3,1},{4,6},{5,7},{6,4},{7,5},{8,10},{9,11},{10,... | collective-permute-start | bytes 55304 | tf_op jit(solution)/shard_map/ppermute | solution.py:374
  119.7 5.5 %collective-permute-start.9 = (f32[72,64]{1,0:T(8,128)S(1)}, f32[72,64]{1,0:T(8,128)S(1)}, u32[]{:S(2)}, u32[]{:S(2)}) collective-permute-start(f32[72,64]{1,0:T(8,128)S(1)} %add.65), channel_id=1, source_target_pairs={{0,4},{1,5},{2,6},{3,7},{4,0},{5,1},{6,2},{7,3},{8,12},{9,13},{10,... | collective-permute-start | bytes 55304 | tf_op jit(solution)/shard_map/ppermute | solution.py:374
  125.2 5.5 %collective-permute-start.10 = (f32[72,64]{1,0:T(8,128)S(1)}, f32[72,64]{1,0:T(8,128)S(1)}, u32[]{:S(2)}, u32[]{:S(2)}) collective-permute-start(f32[72,64]{1,0:T(8,128)S(1)} %add.66), channel_id=1, source_target_pairs={{0,8},{1,9},{2,10},{3,11},{4,12},{5,13},{6,14},{7,15},{8,0},{9,1},... | collective-permute-start | bytes 55304 | tf_op jit(solution)/shard_map/ppermute | solution.py:374
